TPU v7x, 32 devices: a whole 2x2x4 slice. The times are simulated.
32 devices in a mesh: dp: 16 (over z, y, x), fsdp: 2 (over core).
Axes of the slice: x: 2, y: 2, z: 4, core: 2. Of those that a mesh axis runs over, the one named last changes fastest.
Arguments:
- token_ids: int32 [64, 512], P(('dp', 'fsdp')), may hold values from 0 to 250111, as said below
- seq_lengths: int32 [64], P(('dp', 'fsdp')), may hold values from 128 to 512, as said below
- embedding: float32 [250112, 768], P('dp', 'fsdp'), may hold values from -6 to 6
- embed_rows: float32 [250112], replicated, may hold values from 1e-08 to 2e-06
- embed_cols: float32 [768], replicated, may hold values from 2e-08 to 4e-07
- layers: float32 [1, 768, 9216], P(None, 'dp', 'fsdp'), may hold values from -6 to 6
- layer_rows: float32 [1, 6, 768], replicated, may hold values from 0.0001 to 0.1
- layer_cols: float32 [1, 9216], replicated, may hold values from 0.0001 to 0.1
- head_weight: float32 [768, 768], replicated, may hold values from -0.21875 to 0.21875
- head_rows: float32 [768], replicated, may hold values from 0.0001 to 0.1
- head_cols: float32 [768], replicated, may hold values from 0.0001 to 0.1
- positions: float32 [512, 768], replicated, may hold values from -3 to 3
- pos_rows: float32 [512], replicated, may hold values from 2e-06 to 0.0001
- pos_cols: float32 [768], replicated, may hold values from 2e-06 to 0.0001
- norm_vectors: float32 [14, 768], replicated, may hold values from -1 to 2
- vector_moment: float32 [14, 768], replicated, may hold values from 0.0001 to 0.1
- log_scale: float32 [], replicated, may hold values from 3.4 to 4
- scale_moment: float32 [], replicated, may hold values from 0.01 to 1
Outputs:
- contrast_loss: float32 [], replicated
- embedding_new: float32 [250112, 768], P('dp', 'fsdp')
- embed_rows_new: float32 [250112], replicated
- embed_cols_new: float32 [768], replicated
- embedding_copy: bfloat16 [250112, 768], P('dp', 'fsdp')
- layers_new: float32 [1, 768, 9216], P(None, 'dp', 'fsdp')
- layer_rows_new: float32 [1, 6, 768], replicated
- layer_cols_new: float32 [1, 9216], replicated
- layers_copy: bfloat16 [1, 768, 9216], P(None, 'dp', 'fsdp')
- head_new: float32 [768, 768], replicated
- head_rows_new: float32 [768], replicated
- head_cols_new: float32 [768], replicated
- positions_new: float32 [512, 768], replicated
- pos_rows_new: float32 [512], replicated
- pos_cols_new: float32 [768], replicated
- vectors_new: float32 [14, 768], replicated
- vector_moment_new: float32 [14, 768], replicated
- log_scale_new: float32 [], replicated
- scale_moment_new: float32 [], replicated
- update_rms: float32 [11], replicated
Inputs may be any that keep to these rules, and one draw needn't show every extreme that they name: `token_ids`: in the 2 sequences of each device (aligned blocks of 2 rows), exactly 64 of the 2 x 512 slots hold tokens of each run of 15632 consecutive vocabulary rows. `seq_lengths`: some sequence has exactly 512 tokens.
All inputs are finite; a program needn't handle non-finite values.
Results may differ from a plain program's by a relative error of at most 0.0025.
The roundings to bfloat16 on the way count: a program that leaves them out, or rounds other values in their place, can miss the bound.
Values may be sent and summed in bfloat16 or wider, within the bound.
No kernel may reach another device: no remote copies, remote signals or barrier semaphores. Data moves between devices by JAX's collectives and lax.ppermute only.
A program may use at most 320 MiB of HBM per device.

v0:
```python
import functools
import math

import jax
import jax.numpy as jnp
from jax import lax
from jax.experimental import pallas as pl
from jax.experimental.pallas import tpu as pltpu
from jax.sharding import PartitionSpec as P


MODEL_WIDTH = 768
HEAD = 64
FF = 3072
VOCAB = 250112
MAXLEN = 512
PER_LAYER = 8 + FF // MODEL_WIDTH
COLUMNS = 4 * MODEL_WIDTH + 2 * FF
PIECE = FF // 2
COLORS = 3
TILE_ROWS = 2048

NORM_EPSILON = 1e-05
UNIT_EPSILON = 1e-06
DECAY_RATE = 0.5
FLOOR_SQUARE = 1e-30
FLOOR_SCALE = 0.001
CLIP_LIMIT = 1.0
RELATIVE = 0.3
EXACT_PRECISION = lax.Precision.HIGHEST
BOTH = ("dp", "fsdp")
F32, BF16 = jnp.float32, jnp.bfloat16
CONTRACT_ROWS = (((0,), (0,)), ((), ()))
CONTRACT_COLS = (((1,), (1,)), ((), ()))
CONTRACT_IN = (((1,), (0,)), ((), ()))


def dot(left, right, dims=CONTRACT_IN):
    return lax.dot_general(left, right, dims, preferred_element_type=F32)


def bit_count(size):
    return size.bit_length() - 1


def bit_orders(size):
    count = bit_count(size)
    rest = list(range(count - 1))[::-1]
    turns = [rest[-k:] + rest[:-k] if k else rest for k in range(COLORS)]
    return [[count - 1] + turn for turn in turns]


def sum_orders(size):
    count = bit_count(size)
    top, rest = [count - 1], list(range(count - 1))
    return [rest[:1] + rest[1:][::-1] + top, rest[1:2] + rest[:1] + rest[2:] + top, rest[::-1] + top]


def swap_by(values, axis, size, mask):
    return lax.ppermute(values, axis, [(i, i ^ mask) for i in range(size)])


def swap(values, axis, size, bit):
    return swap_by(values, axis, size, 1 << bit)


def own_bit(axis, bit):
    return (lax.axis_index(axis) >> bit) & 1


def gather_bits(values, axis, size, order):
    count = bit_count(size)
    held = values.reshape((1,) * count + values.shape)
    for bit in order:
        other = swap(held, axis, size, bit)
        dim = count - 1 - bit
        low_first = jnp.concatenate([held, other], dim)
        high_first = jnp.concatenate([other, held], dim)
        held = jnp.where(own_bit(axis, bit) == 0, low_first, high_first)
    return held.reshape((size,) + values.shape)


def in_order(held, size, dim):
    me = lax.axis_index("fsdp")
    for bit in range(bit_count(size)):
        mine = (me >> bit) & 1
        held = [jnp.where(mine == 0, held[k], held[k ^ (1 << bit)]) for k in range(size)]
    return jnp.concatenate(held, dim)


def gather_list(values, axis, size):
    held = [values] + [swap_by(values, axis, size, d) for d in range(1, size)]
    for bit in range(bit_count(size)):
        mine = own_bit(axis, bit)
        held = [jnp.where(mine == 0, held[k], held[k ^ (1 << bit)]) for k in range(size)]
    return held


def fsdp_others(values, size):
    return [swap_by(values, "fsdp", size, d) for d in range(1, size)]


def scatter_bits(values, axis, size, order, dim):
    for place, bit in enumerate(order):
        shape = values.shape
        half = shape[dim] // 2
        above = 1 << sum(1 for b in order[place + 1 :] if b > bit)
        parts = values.reshape(shape[:dim] + (above, 2, half // above) + shape[dim + 1 :])
        mine = own_bit(axis, bit)
        keep = lax.dynamic_index_in_dim(parts, mine, dim + 1, keepdims=False)
        send = lax.dynamic_index_in_dim(parts, 1 - mine, dim + 1, keepdims=False).astype(BF16)
        rest = shape[:dim] + (half,) + shape[dim + 1 :]
        values = keep.reshape(rest) + swap(send.reshape(rest), axis, size, bit).astype(F32)
    return values


def everyone(values, axis, size):
    return lax.all_to_all(
        jnp.broadcast_to(values[None], (size,) + values.shape), axis, 0, 0, tiled=True
    )


def padded(values, multiple):
    return jnp.pad(values, (0, -values.size % multiple))


def attention_scores(query, key_rows, length):
    scores = dot(query, key_rows, CONTRACT_COLS) * 0.125
    valid = lax.broadcasted_iota(jnp.int32, scores.shape, 1) < length
    scores = jnp.where(valid, scores, -1e30)
    raised = jnp.exp(scores - jnp.max(scores, -1, keepdims=True))
    return raised / jnp.sum(raised, -1, keepdims=True)


def attention_kernel(lengths, q_ref, k_ref, v_ref, o_ref):
    length = lengths[pl.program_id(0)]
    lanes = lax.broadcasted_iota(jnp.int32, q_ref.shape, 1)
    query, key_rows, value_rows = q_ref[...], k_ref[...], v_ref[...]
    zero = jnp.zeros_like(query)
    first = attention_scores(jnp.where(lanes < HEAD, query, zero), key_rows, length)
    second = attention_scores(jnp.where(lanes < HEAD, zero, query), key_rows, length)
    out = jnp.where(lanes < HEAD, dot(first.astype(BF16), value_rows), dot(second.astype(BF16), value_rows))
    o_ref[...] = out.astype(BF16)


def attend(lengths, qk, v):
    seqs = lengths.shape[0]
    pairs = MODEL_WIDTH // 128
    block = (MAXLEN, 128)
    return pl.pallas_call(
        attention_kernel,
        grid_spec=pltpu.PrefetchScalarGridSpec(
            num_scalar_prefetch=1,
            grid=(seqs, pairs),
            in_specs=[
                pl.BlockSpec(block, lambda s, h, n: (s, h)),
                pl.BlockSpec(block, lambda s, h, n: (s, h + pairs)),
                pl.BlockSpec(block, lambda s, h, n: (s, h)),
            ],
            out_specs=pl.BlockSpec(block, lambda s, h, n: (s, h)),
        ),
        out_shape=jax.ShapeDtypeStruct((seqs * MAXLEN, MODEL_WIDTH), BF16),
        name="attend",
    )(lengths, qk, qk, v)


def attention_back_kernel(seq, lengths, q_ref, k_ref, v_ref, d_ref, *refs):
    dq_ref, dk_ref, dv_ref, sum_ref = refs[-4:]
    length = lengths[seq]
    lanes = lax.broadcasted_iota(jnp.int32, q_ref.shape, 1)
    query, key_rows, value_rows, d_rows = q_ref[...], k_ref[...], v_ref[...], d_ref[...]
    zero = jnp.zeros_like(query)
    parts = []
    for low_half in (True, False):
        take = (lanes < HEAD) if low_half else (lanes >= HEAD)
        soft = attention_scores(jnp.where(take, query, zero), key_rows, length)
        d_values = dot(soft.astype(BF16), d_rows, CONTRACT_ROWS)
        d_soft = dot(jnp.where(take, d_rows, zero), value_rows, CONTRACT_COLS)
        d_scores = soft * (d_soft - jnp.sum(soft * d_soft, -1, keepdims=True))
        d_low = d_scores.astype(BF16)
        parts.append((dot(d_low, key_rows) * 0.125, dot(d_low, query, CONTRACT_ROWS) * 0.125, d_values))
    dq, dk, dv = (jnp.where(lanes < HEAD, a, b) for a, b in zip(*parts))
    dq_ref[...] = dq.astype(BF16)
    dk_ref[...] = dk.astype(BF16)
    dv_ref[...] = dv.astype(BF16)
    sums = jnp.concatenate([jnp.sum(dq, 0, keepdims=True), jnp.sum(dv, 0, keepdims=True)], 0)
    sum_ref[...] = jnp.concatenate([sums, jnp.zeros((6, 128), F32)], 0)


def attend_back(seq, lengths, qk, v, d_att, before):
    seqs = lengths.shape[0]
    pairs = MODEL_WIDTH // 128
    block = (MAXLEN, 128)
    plain = pl.BlockSpec(block, lambda h, n: (seq, h))
    low = jax.ShapeDtypeStruct((seqs * MAXLEN, MODEL_WIDTH), BF16)
    return pl.pallas_call(
        functools.partial(attention_back_kernel, seq),
        grid_spec=pltpu.PrefetchScalarGridSpec(
            num_scalar_prefetch=1,
            grid=(pairs,),
            in_specs=[plain, pl.BlockSpec(block, lambda h, n: (seq, h + pairs)), plain, plain]
            + [pl.BlockSpec(memory_space=pl.ANY)] * len(before),
            out_specs=[plain, plain, plain, pl.BlockSpec((8, 128), lambda h, n: (seq, h))],
        ),
        out_shape=[low, low, low, jax.ShapeDtypeStruct((seqs * 8, MODEL_WIDTH), F32)],
        input_output_aliases={5 + k: k for k in range(len(before))},
    )(lengths, qk, qk, v, d_att, *before)


def rows_kernel(wanted, table_ref, out_ref, rows, sem):
    count = rows.shape[0]

    def fetch(j, carry):
        pltpu.make_async_copy(table_ref.at[pl.ds(wanted[j], 1)], rows.at[pl.ds(j, 1)], sem).start()
        return carry

    lax.fori_loop(0, count, fetch, 0, unroll=8)
    pltpu.make_async_copy(rows, rows, sem).wait()
    out_ref[...] = rows[...].astype(BF16)


def take_rows(wanted, table):
    count, width = wanted.shape[0], table.shape[1]
    return pl.pallas_call(
        rows_kernel,
        grid_spec=pltpu.PrefetchScalarGridSpec(
            num_scalar_prefetch=1,
            grid=(1,),
            in_specs=[pl.BlockSpec(memory_space=pl.ANY)],
            out_specs=pl.BlockSpec((count, width), lambda i, n: (0, 0)),
            scratch_shapes=[pltpu.VMEM((count, width), F32), pltpu.SemaphoreType.DMA],
        ),
        out_shape=jax.ShapeDtypeStruct((count, width), BF16),
        name="take_rows",
    )(wanted, table)


def table_kernel(rows_at, starts, table_ref, update_ref, scale_ref, new_ref, low_ref):
    tile = pl.program_id(0)
    base = tile * TILE_ROWS
    scale = scale_ref[...]
    new_ref[...] = table_ref[...]

    def patch(k, carry):
        row = pl.ds(rows_at[k] - base, 1)
        new_ref[row, :] = table_ref[row, :] - scale * update_ref[pl.ds(k, 1), :]
        return carry

    lax.fori_loop(starts[tile], starts[tile + 1], patch, 0)
    low_ref[...] = new_ref[...].astype(BF16)


def table_update(rows_at, starts, table, update, scale):
    height, width = table.shape
    tile = pl.BlockSpec((TILE_ROWS, width), lambda i, *_: (i, 0))
    return pl.pallas_call(
        table_kernel,
        grid_spec=pltpu.PrefetchScalarGridSpec(
            num_scalar_prefetch=2,
            grid=(pl.cdiv(height, TILE_ROWS),),
            in_specs=[
                tile,
                pl.BlockSpec(update.shape, lambda i, *_: (0, 0)),
                pl.BlockSpec(scale.shape, lambda i, *_: (0, 0)),
            ],
            out_specs=[tile, tile],
        ),
        out_shape=[
            jax.ShapeDtypeStruct((height, width), F32),
            jax.ShapeDtypeStruct((height, width), BF16),
        ],
        name="table_update",
    )(rows_at, starts, table, update, scale)


def norm_forward(values, gain_row, bias_row):
    center = values - jnp.mean(values, -1, keepdims=True)
    spread = jnp.mean(center * center, -1, keepdims=True)
    inverse = lax.rsqrt(spread + NORM_EPSILON)
    unit = center * inverse
    return unit * gain_row + bias_row, (unit, inverse)


def norm_backward(d_out, kept, gain_row):
    unit, inverse = kept
    scaled = d_out * gain_row
    d_in = inverse * (
        scaled - jnp.mean(scaled, -1, keepdims=True) - unit * jnp.mean(scaled * unit, -1, keepdims=True)
    )
    return d_in, jnp.sum(d_out * unit, 0), jnp.sum(d_out, 0)


def gelu_and_slope(values):
    normal = 0.5 + 0.5 * lax.erf(values * math.sqrt(0.5))
    slope = normal + values * (jnp.exp(-0.5 * values * values) * (1.0 / math.sqrt(2.0 * math.pi)))
    return values * normal, slope


def exact(left, right, dims=CONTRACT_IN):
    return lax.dot_general(left, right, dims, precision=EXACT_PRECISION, preferred_element_type=F32)


def contrast_kernel(scale_ref, pooled_ref, head_ref, d_pooled_ref, d_projected_ref, loss_ref):
    projected = exact(pooled_ref[...], head_ref[...])
    inverse = lax.rsqrt(jnp.sum(projected * projected, -1, keepdims=True) + UNIT_EPSILON)
    units = projected * inverse
    scale = jnp.exp(jnp.full((1, 1), scale_ref[0], F32))
    logits = scale * exact(units, units, CONTRACT_COLS)
    row = lax.broadcasted_iota(jnp.int32, logits.shape, 0)
    col = lax.broadcasted_iota(jnp.int32, logits.shape, 1)
    used = (row % 2 == 0) & (col % 2 == 1)
    pairs = used & (col == row + 1)
    total = jnp.zeros((1, 1), F32)
    d_logits = jnp.where(pairs, -1.0, 0.0)
    for axis in (1, 0):
        seen = jnp.where(used, logits, -1e30)
        peak = jnp.max(seen, axis, keepdims=True)
        raised = jnp.where(used, jnp.exp(seen - peak), 0.0)
        sums = jnp.sum(raised, axis, keepdims=True)
        safe = jnp.where(sums > 0.0, sums, 1.0)
        d_logits += 0.5 * raised / safe
        logs = jnp.where(sums > 0.0, peak + jnp.log(safe), 0.0)
        total += 0.5 * jnp.sum(jnp.sum(logs, 1, keepdims=True), 0, keepdims=True)
    matched = jnp.where(pairs, logits, 0.0)
    total -= jnp.sum(jnp.sum(matched, 1, keepdims=True), 0, keepdims=True)
    weighted = jnp.where(used, d_logits * logits, 0.0)
    d_scale = jnp.sum(jnp.sum(weighted, 1, keepdims=True), 0, keepdims=True)
    d_units = scale * (exact(d_logits, units) + exact(d_logits, units, CONTRACT_ROWS))
    along = jnp.sum(projected * d_units, -1, keepdims=True)
    d_projected = inverse * d_units - projected * (inverse * inverse * inverse * along)
    d_projected_ref[...] = d_projected
    d_pooled_ref[...] = exact(d_projected, head_ref[...], CONTRACT_COLS)
    lane = lax.broadcasted_iota(jnp.int32, (8, 128), 1)
    loss_ref[...] = jnp.where(lane == 0, total, jnp.where(lane == 1, d_scale, 0.0))


def contrast(pooled, head_weight, log_scale):
    vmem = pl.BlockSpec(memory_space=pltpu.VMEM)
    like = jax.ShapeDtypeStruct(pooled.shape, F32)
    return pl.pallas_call(
        contrast_kernel,
        in_specs=[pl.BlockSpec(memory_space=pltpu.SMEM), vmem, vmem],
        out_specs=[vmem] * 3,
        out_shape=[like, like, jax.ShapeDtypeStruct((8, 128), F32)],
        name="contrast",
    )(log_scale.reshape(1), pooled, head_weight)


def factored_step(gradient, rows_old, cols_old):
    square = gradient * gradient
    rows_new = DECAY_RATE * rows_old + (1.0 - DECAY_RATE) * (jnp.mean(square, 1) + FLOOR_SQUARE)
    cols_new = DECAY_RATE * cols_old + (1.0 - DECAY_RATE) * (jnp.mean(square, 0) + FLOOR_SQUARE)
    estimate = rows_new[:, None] * cols_new[None, :] / jnp.mean(rows_new)
    return (gradient * lax.rsqrt(estimate), rows_new, cols_new)


def plain_step(gradient, moment_old):
    moment_new = DECAY_RATE * moment_old + (1.0 - DECAY_RATE) * (gradient * gradient + FLOOR_SQUARE)
    return (gradient * lax.rsqrt(moment_new), moment_new)


def apply_update(weight_matrix, update):
    spread = jnp.sqrt(jnp.mean(update * update))
    clip_factor = jnp.maximum(1.0, spread / CLIP_LIMIT)
    step_size = RELATIVE * jnp.maximum(FLOOR_SCALE, jnp.sqrt(jnp.mean(weight_matrix * weight_matrix)))
    return (weight_matrix - step_size * (update / clip_factor), spread)


def body(
    token_ids,
    seq_lengths,
    embedding,
    embed_rows,
    embed_cols,
    layers,
    layer_rows,
    layer_cols,
    head_weight,
    head_rows,
    head_cols,
    positions,
    pos_rows,
    pos_cols,
    norm_vectors,
    vector_moment,
    log_scale,
    scale_moment,
):
    outer = lax.axis_size("dp")
    inner = lax.axis_size("fsdp")
    devices = outer * inner
    outer_index = lax.axis_index("dp")
    inner_index = lax.axis_index("fsdp")
    seq_count = token_ids.shape[0]
    slots = seq_count * MAXLEN
    cap = slots // outer
    shard_rows, shard_cols = embedding.shape
    local_rows, local_cols = layers.shape[1], layers.shape[2]
    gather_orders = bit_orders(outer)
    scatter_orders = [order[::-1] for order in gather_orders]
    block_orders = sum_orders(outer)
    inner_order = list(range(bit_count(inner)))

    flat = token_ids.reshape(slots)
    owners = flat // shard_rows
    offsets = flat - owners * shard_rows
    hot = owners[:, None] == jnp.arange(outer, dtype=jnp.int32)[None, :]
    counting = jnp.arange(slots, dtype=jnp.int32)
    before = dot((counting[:, None] >= counting[None, :]).astype(BF16), hot.astype(BF16))
    rank = jnp.sum(jnp.where(hot, before, 0.0), 1).astype(jnp.int32) - 1
    bucket = owners * cap + rank
    outgoing = jnp.sum(jnp.where(counting[:, None] == bucket[None, :], offsets[None, :], 0), 1)
    asked = lax.all_to_all(outgoing.reshape(outer, cap), "dp", 0, 0, tiled=True)
    wanted = jnp.stack([asked] + fsdp_others(asked, inner), 1).reshape(-1)
    entries = wanted.shape[0]

    wanted, forward_vectors, forward_positions, lengths = lax.optimization_barrier(
        (wanted, norm_vectors, positions, seq_lengths.astype(jnp.int32))
    )

    old_rows_mean = jnp.mean(embed_rows)

    low_layers = layers[0].astype(BF16)
    width = local_cols // COLORS
    gathered = []
    for color in range(COLORS):
        piece = low_layers[:, color * width : (color + 1) * width]
        whole = gather_bits(piece, "dp", outer, gather_orders[color]).reshape(MODEL_WIDTH, width)
        gathered.append(gather_list(whole, "fsdp", inner))
    pieces = [gathered[color][f] for f in range(inner) for color in range(COLORS)]
    group = PIECE // width
    weights = [
        pieces[k] if group == 1 else jnp.concatenate(pieces[k * group : (k + 1) * group], 1)
        for k in range(COLUMNS // PIECE)
    ]
    w_qk, w_vo, w_up, w_down = weights[0], weights[1], weights[2:4], weights[4:6]
    w_v, w_o = w_vo[:, :MODEL_WIDTH], w_vo[:, MODEL_WIDTH:]

    looked = take_rows(wanted, embedding).reshape(outer, inner, cap, shard_cols)
    replies = lax.all_to_all(looked, "dp", 0, 0, tiled=True)
    own_part = replies[:, 0].reshape(slots, shard_cols)
    other_parts = [swap_by(replies[:, d].reshape(slots, shard_cols), "fsdp", inner, d) for d in range(1, inner)]
    rows_low = in_order([own_part] + other_parts, inner, 1)
    token_rows = dot((bucket[:, None] == counting[None, :]).astype(BF16), rows_low)

    embedded = (token_rows.reshape(seq_count, MAXLEN, MODEL_WIDTH) + forward_positions[None]).reshape(slots, MODEL_WIDTH)
    vectors = forward_vectors[2 : 2 + PER_LAYER]
    bias_q, bias_v, bias_o, bias_d, gain_one, bias_one, gain_two, bias_two = (vectors[k] for k in range(8))
    bias_up = vectors[8:].reshape(2, PIECE)
    hidden, kept_zero = norm_forward(embedded, forward_vectors[0], forward_vectors[1])
    hidden_low = hidden.astype(BF16)
    qk = (dot(hidden_low, w_qk) + jnp.concatenate([bias_q, jnp.zeros_like(bias_q)])).astype(BF16)
    v = (dot(hidden_low, w_v) + bias_v).astype(BF16)
    attended = attend(lengths, qk, v)
    first, kept_one = norm_forward(hidden + (dot(attended, w_o) + bias_o), gain_one, bias_one)
    first_low = first.astype(BF16)
    active, slopes = [], []
    for k in range(2):
        value, slope = gelu_and_slope(dot(first_low, w_up[k]) + bias_up[k])
        active.append(value.astype(BF16))
        slopes.append(slope)
    downward = dot(active[0], w_down[0], CONTRACT_COLS) + dot(active[1], w_down[1], CONTRACT_COLS) + bias_d
    final, kept_two = norm_forward(first + downward, gain_two, bias_two)

    valid = (jnp.arange(MAXLEN)[None, :] < lengths[:, None]).astype(F32)
    lengths_float = lengths.astype(F32)[:, None]
    pooled = jnp.sum(final.reshape(seq_count, MAXLEN, MODEL_WIDTH) * valid[:, :, None], 1) / lengths_float
    all_pooled = everyone(pooled, BOTH, devices).reshape(devices * seq_count, MODEL_WIDTH)
    d_all_pooled, d_projected, loss_out = contrast(all_pooled, head_weight, log_scale)
    loss_value, grad_scale = loss_out[0, 0], loss_out[0, 1]
    device_index = outer_index * inner + inner_index
    d_pooled = lax.dynamic_slice_in_dim(d_all_pooled, device_index * seq_count, seq_count, 0)
    d_final = ((d_pooled / lengths_float)[:, None, :] * valid[:, :, None]).reshape(slots, MODEL_WIDTH)

    def columns_sum(make, whole):
        if inner != 2:
            return scatter_bits(whole(), "fsdp", inner, inner_order[::-1], 1)
        sent = swap(make(1 - inner_index).astype(BF16), "fsdp", 2, 0)
        return make(inner_index) + sent.astype(F32)

    def rows_sum(values, order):
        return scatter_bits(values, "dp", outer, order, 0)

    def of_two(half, pair):
        return jnp.where(half == 0, pair[0], pair[1])

    def half_columns(half, values):
        return lax.dynamic_slice_in_dim(values, half * (values.shape[1] // 2), values.shape[1] // 2, 1)

    d_two, d_gain_two, d_bias_two = norm_backward(d_final, kept_two, gain_two)
    d_two_low = d_two.astype(BF16)
    part_down = columns_sum(
        lambda half: dot(d_two_low, of_two(half, active), CONTRACT_ROWS),
        lambda: jnp.concatenate([dot(d_two_low, active[k], CONTRACT_ROWS) for k in range(2)], 1),
    )
    sum_down = rows_sum(part_down, block_orders[0])
    d_ups = [slopes[k] * dot(d_two_low, w_down[k]) for k in range(2)]
    d_up_lows = [d_up.astype(BF16) for d_up in d_ups]
    part_up = columns_sum(
        lambda half: dot(first_low, of_two(half, d_up_lows), CONTRACT_ROWS),
        lambda: jnp.concatenate([dot(first_low, d_up_lows[k], CONTRACT_ROWS) for k in range(2)], 1),
    )
    sum_up = rows_sum(part_up, block_orders[1])
    d_first = d_two + dot(d_up_lows[0], w_up[0], CONTRACT_COLS) + dot(d_up_lows[1], w_up[1], CONTRACT_COLS)
    d_one, d_gain_one, d_bias_one = norm_backward(d_first, kept_one, gain_one)
    d_one_low = d_one.astype(BF16)
    d_attended = dot(d_one_low, w_o, CONTRACT_COLS).astype(BF16)
    part_out = columns_sum(
        lambda half: dot(attended, half_columns(half, d_one_low), CONTRACT_ROWS),
        lambda: dot(attended, d_one_low, CONTRACT_ROWS),
    )
    sum_out = rows_sum(part_out, block_orders[2])
    d_heads = ()
    for seq in range(seq_count):
        d_heads = attend_back(seq, lengths, qk, v, d_attended, d_heads)
    d_q, d_k, d_v, d_sums = d_heads
    d_hidden = (
        d_one
        + dot(d_q, w_qk[:, :MODEL_WIDTH], CONTRACT_COLS)
        + dot(d_k, w_qk[:, MODEL_WIDTH:], CONTRACT_COLS)
        + dot(d_v, w_v, CONTRACT_COLS)
    )
    d_embedded, d_gain_zero, d_bias_zero = norm_backward(d_hidden, kept_zero, forward_vectors[0])

    d_tokens = d_embedded.astype(BF16)
    back_rows = dot((counting[:, None] == bucket[None, :]).astype(BF16), d_tokens).astype(BF16)
    parts = [
        lax.dynamic_slice_in_dim(back_rows, (inner_index ^ d) * shard_cols, shard_cols, 1) for d in range(inner)
    ]
    parts = parts[:1] + [swap_by(parts[d], "fsdp", inner, d) for d in range(1, inner)]
    back = jnp.concatenate([rows.reshape(outer, 1, cap, shard_cols) for rows in parts], 1)
    (
        back,
        embed_rows,
        embed_cols,
        layer_rows,
        layer_cols,
        layers,
        head_weight,
        head_rows,
        head_cols,
        positions,
        pos_rows,
        pos_cols,
        norm_vectors,
        vector_moment,
        all_pooled,
        d_projected,
    ) = lax.optimization_barrier(
        (
            back,
            embed_rows,
            embed_cols,
            layer_rows,
            layer_cols,
            layers,
            head_weight,
            head_rows,
            head_cols,
            positions,
            pos_rows,
            pos_cols,
            norm_vectors,
            vector_moment,
            all_pooled,
            d_projected,
        )
    )
    returned = lax.all_to_all(back, "dp", 0, 0, tiled=True).reshape(entries, shard_cols)

    d_positions = jnp.sum(d_embedded.reshape(seq_count, MAXLEN, MODEL_WIDTH), 0)
    part = MODEL_WIDTH // inner
    part_positions = columns_sum(lambda half: half_columns(half, d_positions), lambda: d_positions)
    reduced = []
    for color, d_rows in enumerate((d_q, d_k, d_v)):
        block = columns_sum(
            lambda half: dot(hidden_low, half_columns(half, d_rows), CONTRACT_ROWS),
            lambda: dot(hidden_low, d_rows, CONTRACT_ROWS),
        ).reshape(outer, local_rows, part)
        if color == 0:
            block = jnp.concatenate([block, part_positions.reshape(outer, MAXLEN // outer, part)], 1)
        reduced.append(rows_sum(block, scatter_orders[color])[0])
    own_positions = reduced[0][local_rows:]
    reduced[0] = reduced[0][:local_rows]
    sums = d_sums.reshape(seq_count, 8, MODEL_WIDTH).sum(0)
    d_vectors = jnp.concatenate(
        [
            d_gain_zero,
            d_bias_zero,
            sums[0],
            sums[1],
            jnp.sum(d_one, 0),
            jnp.sum(d_two, 0),
            d_gain_one,
            d_bias_one,
            d_gain_two,
            d_bias_two,
            jnp.sum(d_ups[0], 0),
            jnp.sum(d_ups[1], 0),
        ]
    )
    vector_share = d_vectors.size // devices

    def to_columns(values):
        whole = gather_list(values, "fsdp", inner)
        return lambda low, high: jnp.concatenate([piece[:, low:high] for piece in whole], 1)

    early = to_columns(jnp.concatenate([sum_out, sum_up, sum_down], 1))
    late = to_columns(jnp.concatenate(reduced, 1))
    cut = [0, part, part + FF // inner, part + 2 * FF // inner]
    full_grad = jnp.concatenate(
        [late(k * part, (k + 1) * part) for k in range(3)] + [early(cut[k], cut[k + 1]) for k in range(3)], 1
    )
    grad_layers = lax.dynamic_slice_in_dim(full_grad, inner_index * local_cols, local_cols, 1)

    entry = jnp.arange(entries, dtype=jnp.int32)
    goes_before = (wanted[None, :] < wanted[:, None]) | (
        (wanted[None, :] == wanted[:, None]) & (entry[None, :] < entry[:, None])
    )
    rank = jnp.sum(goes_before.astype(jnp.int32), 1)
    rows_at = jnp.sum(jnp.where(rank[None, :] == entry[:, None], wanted[None, :], 0), 1)
    is_first = jnp.concatenate([jnp.ones((1,), bool), rows_at[1:] != rows_at[:-1]]).astype(F32)
    tiles = -(-shard_rows // TILE_ROWS)
    starts = jnp.sum(
        (rows_at[None, :] < (jnp.arange(tiles + 1, dtype=jnp.int32) * TILE_ROWS)[:, None]).astype(jnp.int32), 1
    )
    lanes = 128
    high, low_digit = rows_at // lanes, rows_at % lanes
    digits = -(-shard_rows // lanes)
    high_hot = (jnp.arange(digits, dtype=jnp.int32)[:, None] == high[None, :]).astype(F32)
    low_hot = (low_digit[:, None] == jnp.arange(lanes, dtype=jnp.int32)[None, :]).astype(F32)
    own_rows_old = lax.dynamic_slice_in_dim(embed_rows, outer_index * shard_rows, shard_rows)
    dense_old = jnp.pad(own_rows_old, (0, digits * lanes - shard_rows)).reshape(digits, lanes)
    picked = lax.dot_general(high_hot, dense_old, CONTRACT_ROWS, precision=EXACT_PRECISION)
    entry_rows_old = jnp.sum(picked * low_hot, 1)
    embed_square = jnp.sum(embedding * embedding)

    grad_rows = dot((rows_at[:, None] == wanted[None, :]).astype(BF16), returned)
    row_part = jnp.sum(grad_rows * grad_rows, 1)
    row_sums = row_part
    for bit in inner_order:
        row_sums = row_sums + swap(row_sums, "fsdp", inner, bit)
    entry_rows = DECAY_RATE * entry_rows_old + (1.0 - DECAY_RATE) * (row_sums / MODEL_WIDTH + FLOOR_SQUARE)
    scaled_rows = grad_rows * lax.rsqrt(entry_rows)[:, None]
    col_part = jnp.sum(grad_rows * grad_rows * is_first[:, None], 0)
    scaled_part = jnp.sum(scaled_rows * scaled_rows * is_first[:, None], 0)
    common = jnp.concatenate([col_part, scaled_part, jnp.sum(row_part * is_first)[None], embed_square[None]])
    payload = jnp.concatenate(
        [
            jnp.broadcast_to(common[None], (devices, common.size)),
            d_vectors.reshape(devices, vector_share),
        ],
        1,
    )
    payload = jnp.pad(payload, ((0, 0), (0, -payload.shape[1] % 1024))).reshape(devices, -1, 128)
    stats = lax.all_to_all(payload, BOTH, 0, 0, tiled=True).reshape(devices, -1)
    own_vectors = jnp.sum(stats[:, common.size : common.size + vector_share], 0)
    embed_stats = own_vectors
    stats = stats[:, : common.size].reshape(outer, inner, common.size).sum(0)
    embed_col_sum = stats[:, :shard_cols].reshape(-1)
    scaled_sum = stats[:, shard_cols : 2 * shard_cols].reshape(-1)
    embed_total, embed_squares = jnp.sum(stats[:, -2]), jnp.sum(stats[:, -1])
    embed_cols_new = DECAY_RATE * embed_cols + (1.0 - DECAY_RATE) * (embed_col_sum / VOCAB + FLOOR_SQUARE)
    rows_mean = DECAY_RATE * old_rows_mean + (1.0 - DECAY_RATE) * (
        embed_total / MODEL_WIDTH / VOCAB + FLOOR_SQUARE
    )
    count = float(VOCAB * MODEL_WIDTH)
    embed_spread = jnp.sqrt(jnp.sum(scaled_sum * (rows_mean / embed_cols_new)) / count)
    embed_step = RELATIVE * jnp.maximum(FLOOR_SCALE, jnp.sqrt(embed_squares / count))
    embed_scale = embed_step / jnp.maximum(1.0, embed_spread / CLIP_LIMIT)
    own_cols = lax.dynamic_slice_in_dim(embed_cols_new, inner_index * shard_cols, shard_cols)
    col_scale = embed_scale * lax.rsqrt(own_cols / rows_mean)
    embedding_new, embedding_copy = table_update(rows_at, starts, embedding, scaled_rows, col_scale[None])
    dense_rows = jnp.dot(
        high_hot, low_hot * (row_sums * is_first)[:, None], precision=EXACT_PRECISION
    ).reshape(-1)

    unit = math.gcd(local_cols, MODEL_WIDTH)
    groups = local_cols // unit
    bounds = [0, 1, 2, 3, 4, 4 + FF // MODEL_WIDTH, 4 + 2 * FF // MODEL_WIDTH]
    bounds = [b * (MODEL_WIDTH // unit) for b in bounds]
    widths = jnp.array([MODEL_WIDTH] * 4 + [FF] * 2, F32)

    def by_block(values):
        return jnp.stack([jnp.sum(values[..., bounds[b] : bounds[b + 1]], -1) for b in range(6)], -1)

    def by_group(values):
        return jnp.stack([jnp.sum(values[..., g * unit : (g + 1) * unit], -1) for g in range(groups)], -1)

    def own_groups(block_values):
        per_group = jnp.stack([block_values[..., b] for b in range(6) for _ in range(bounds[b + 1] - bounds[b])], -1)
        return lax.dynamic_slice_in_dim(per_group, inner_index * groups, groups, per_group.ndim - 1)

    def over_columns(group_values, columns):
        return jnp.concatenate(
            [jnp.broadcast_to(group_values[:, g : g + 1], (group_values.shape[0], unit)) for g in range(columns)], 1
        )

    layer_square = grad_layers * grad_layers
    row_groups = by_group(layer_square)
    all_groups = jnp.concatenate(gather_list(row_groups, "fsdp", inner), 1)
    own_row_sums = by_block(all_groups)
    own_rows_before = lax.dynamic_slice_in_dim(layer_rows[0], outer_index * local_rows, local_rows, 1)
    own_layer_rows = DECAY_RATE * own_rows_before.T + (1.0 - DECAY_RATE) * (
        own_row_sums / widths[None, :] + FLOOR_SQUARE
    )
    scaled_grad = grad_layers * over_columns(lax.rsqrt(own_groups(own_layer_rows)), groups)
    weight_groups = jnp.sum(by_group(layers[0] * layers[0]), 0)
    lead = 1024
    payload = jnp.concatenate(
        [
            padded(jnp.concatenate([own_row_sums.reshape(-1), weight_groups]), lead),
            jnp.sum(layer_square, 0),
            jnp.sum(scaled_grad * scaled_grad, 0),
        ]
    )
    payload, _ = lax.optimization_barrier((payload, embed_stats))
    stats = everyone(payload.reshape(-1, 128), "dp", outer).reshape(outer, -1)
    row_stats = stats[:, : local_rows * 6].reshape(MODEL_WIDTH, 6)
    layer_rows_new = DECAY_RATE * layer_rows[0] + (1.0 - DECAY_RATE) * (
        row_stats.T / widths[:, None] + FLOOR_SQUARE
    )
    col_stats = jnp.sum(stats[:, local_rows * 6 :], 0)
    own_weight_groups, col_stats = col_stats[:groups], col_stats[lead - local_rows * 6 :]
    own_cols_before = lax.dynamic_slice_in_dim(layer_cols[0], inner_index * local_cols, local_cols, 0)
    own_layer_cols = DECAY_RATE * own_cols_before + (1.0 - DECAY_RATE) * (
        col_stats[:local_cols] / MODEL_WIDTH + FLOOR_SQUARE
    )
    rows_means = jnp.mean(layer_rows_new, -1)
    ratio = col_stats[local_cols:] / own_layer_cols
    own_share = jnp.stack([jnp.sum(ratio[g * unit : (g + 1) * unit]) for g in range(groups)])
    shares = gather_list(padded(jnp.concatenate([own_layer_cols, own_share, own_weight_groups]), 1024), "fsdp", inner)
    layer_cols_new = jnp.concatenate([values[:local_cols] for values in shares])
    update_groups = jnp.concatenate([values[local_cols : local_cols + groups] for values in shares])
    weight_groups = jnp.concatenate([values[local_cols + groups : local_cols + 2 * groups] for values in shares])
    counts = MODEL_WIDTH * widths
    spreads = jnp.sqrt(by_block(update_groups) * rows_means / counts)
    layer_scale = (
        RELATIVE
        * jnp.maximum(FLOOR_SCALE, jnp.sqrt(by_block(weight_groups) / counts))
        / jnp.maximum(1.0, spreads / CLIP_LIMIT)
    )
    group_scale = own_groups(layer_scale * jnp.sqrt(rows_means))
    col_factor = (lax.rsqrt(own_layer_cols).reshape(groups, unit) * group_scale[:, None]).reshape(1, local_cols)
    layers_new = layers[0] - scaled_grad * col_factor

    own_dense = dense_rows[:shard_rows]
    share = -(-shard_rows // inner)
    dense_pad = jnp.pad(own_dense, (0, share * inner - shard_rows))
    own_share = lax.dynamic_slice_in_dim(dense_pad, inner_index * share, share)
    flat_part = padded(jnp.concatenate([own_vectors, own_share]), 8 * part).reshape(-1, part)
    pos_rows_count = own_positions.shape[0]
    payload, _ = lax.optimization_barrier((jnp.concatenate([own_positions, flat_part], 0), stats))
    spread = everyone(payload, "dp", outer)
    spread = gather_list(spread, "fsdp", inner)
    grad_pos = jnp.concatenate([values[:, :pos_rows_count].reshape(MAXLEN, part) for values in spread], 1)
    flats = [values[:, pos_rows_count:].reshape(outer, -1) for values in spread]
    grad_vectors = jnp.stack([values[:, :vector_share] for values in flats], 1).reshape(norm_vectors.shape)
    embed_row_sum = jnp.concatenate([values[:, vector_share : vector_share + share] for values in flats], 1)
    embed_row_sum = embed_row_sum[:, :shard_rows].reshape(-1)
    embed_rows_new = DECAY_RATE * embed_rows + (1.0 - DECAY_RATE) * (embed_row_sum / MODEL_WIDTH + FLOOR_SQUARE)

    grad_head = lax.dot_general(all_pooled, d_projected, CONTRACT_ROWS, precision=EXACT_PRECISION)
    head_update, head_rows_new, head_cols_new = factored_step(grad_head, head_rows, head_cols)
    head_new, head_spread = apply_update(head_weight, head_update)
    pos_update, pos_rows_new, pos_cols_new = factored_step(grad_pos, pos_rows, pos_cols)
    positions_new, pos_spread = apply_update(positions, pos_update)
    vector_update, vector_moment_new = plain_step(grad_vectors, vector_moment)
    vectors_new, vector_spread = apply_update(norm_vectors, vector_update)
    scale_update, scale_moment_new = plain_step(grad_scale, scale_moment)
    log_scale_new, scale_spread = apply_update(log_scale, scale_update)
    update_rms = jnp.concatenate(
        [jnp.stack([embed_spread, head_spread, pos_spread, vector_spread, scale_spread]), spreads]
    )
    return (
        loss_value,
        embedding_new,
        embed_rows_new,
        embed_cols_new,
        embedding_copy,
        layers_new[None],
        layer_rows_new[None],
        layer_cols_new[None],
        layers_new.astype(BF16)[None],
        head_new,
        head_rows_new,
        head_cols_new,
        positions_new,
        pos_rows_new,
        pos_cols_new,
        vectors_new,
        vector_moment_new,
        log_scale_new,
        scale_moment_new,
        update_rms,
    )


def solution(mesh):
    split = P("dp", "fsdp")
    layer_split = P(None, "dp", "fsdp")
    whole = P()
    return jax.shard_map(
        body,
        mesh=mesh,
        in_specs=(P(BOTH, None), P(BOTH), split, whole, whole, layer_split) + (whole,) * 12,
        out_specs=(whole, split, whole, whole, split, layer_split, whole, whole, layer_split) + (whole,) * 11,
        check_vma=False,
    )
```

profile of v0, /device:TPU:0, one launch (start us, length us, event | category | flops | bytes accessed | tf_op | source)
XLA Modules:
  0.0 708.5 jit_solution(18392493916088097548)
XLA Ops:
  3.1 8.3 %all-to-all-start = ((s32[16,1,64]{2,1,0:T(1,128)}), s32[16,1,64]{2,1,0:T(1,128)S(1)}, u32[]{:S(2)}, u32[]{:S(2)}) async-start(s32[16,1,64]{2,1,0:T(1,128)} %all_to_all.26), calls=%async_computation | async-start | bytes 16384 | tf_op jit(solution)/shard_map/all_to_all | solution.py:413
  18.5 11.8 %multiply_reduce_fusion = f32[]{:T(128)} fusion(f32[15632,384]{1,0:T(8,128)} %table_ref.3), kind=kLoop, calls=%fused_computation | loop fusion | flops 12005375 | bytes 24010756 | tf_op jit(solution)/shard_map/reduce_sum | solution.py:636
  33.9 14.4 %take_rows.1 = bf16[2048,384]{1,0:T(8,128)(2,1)} custom-call(s32[2048]{0:T(1024)} %reshape.2145.wanted, f32[15632,384]{1,0:T(8,128)} %table_ref.3), custom_call_target="tpu_custom_call" | custom-call | tf_op jit(solution)/shard_map/take_rows/pallas_call | solution.py:224
  48.4 5.2 convert_reduce_fusion
  53.6 5.0 all-to-all-start.1
  65.8 7.0 collective-permute-done.8
  74.0 31.8 %collective-permute-done.9 = bf16[2,1,1,2,48,1536]{5,4,0,3,2,1:T(8,128)(2,1)S(1)} collective-permute-done((bf16[2,1,1,2,48,1536]{5,4,0,3,2,1:T(8,128)(2,1)S(1)}, bf16[2,1,1,2,48,1536]{5,4,0,3,2,1:T(8,128)(2,1)S(1)}, u32[]{:S(2)}, u32[]{:S(2)}) %collective-permute-start.9) | collective-permute-done | bytes 589856 | tf_op jit(solution)/shard_map/ppermute | solution.py:60
  110.0 36.6 %collective-permute-done.4 = bf16[2,2,1,1,48,1536]{5,4,3,2,1,0:T(8,128)(2,1)S(1)} collective-permute-done((bf16[2,2,1,1,48,1536]{5,4,3,2,1,0:T(8,128)(2,1)S(1)}, bf16[2,2,1,1,48,1536]{5,4,3,2,1,0:T(8,128)(2,1)S(1)}, u32[]{:S(2)}, u32[]{:S(2)}) %collective-permute-start.4) | collective-permute-done | bytes 589856 | tf_op jit(solution)/shard_map/ppermute | solution.py:60
  152.0 21.5 %collective-permute-done.5 = bf16[2,2,2,1,48,1536]{5,4,3,2,1,0:T(8,128)(2,1)} collective-permute-done((bf16[2,2,2,1,48,1536]{5,4,3,2,1,0:T(8,128)(2,1)S(1)}, bf16[2,2,2,1,48,1536]{5,4,3,2,1,0:T(8,128)(2,1)}, u32[]{:S(2)}, u32[]{:S(2)}) %collective-permute-start.5) | collective-permute-done | bytes 1179680 | tf_op jit(solution)/shard_map/ppermute | solution.py:60
  175.6 3.8 collective-permute-done.15
  179.4 4.5 maximum_select_fusion.2
  188.8 3.6 broadcast_select_fusion.4
  197.8 4.5 add_convert_fusion.q_ref.k_ref
  202.3 15.8 %attend.1 = bf16[1024,768]{1,0:T(8,128)(2,1)} custom-call(s32[2]{0:T(128)} %lengths.2, bf16[1024,1536]{1,0:T(8,128)(2,1)} %add_convert_fusion.q_ref.k_ref, bf16[1024,1536]{1,0:T(8,128)(2,1)} %add_convert_fusion.q_ref.k_ref, bf16[1024,768]{1,0:T(8,128)(2,1)} %add_convert_fusion.1.v_ref), custom_call_target="tpu_custom_call" | custom-call | tf_op jit(solution)/shard_map/attend/pallas_call | solution.py:150
  225.0 5.4 multiply_convert_fusion
  230.4 6.9 multiply_convert_fusion.1
  237.3 5.4 fusion.82
  242.8 4.9 fusion.182
  249.9 5.0 all-to-all-start.2
  257.0 6.9 all-to-all-done.2
  264.6 8.0 %contrast.1 = (f32[64,768]{1,0:T(8,128)}, f32[64,768]{1,0:T(8,128)}, f32[8,128]{1,0:T(8,128)}) custom-call(f32[1]{0:T(128)} %bitcast.383.scale_ref, f32[64,768]{1,0:T(8,128)} %reshape.2151.pooled_ref, f32[768,768]{1,0:T(8,128)} %head_ref.1), custom_call_target="tpu_custom_call" | custom-call | tf_op jit(solution)/shard_map/contrast/pallas_call | solution.py:340
  278.8 4.1 convolution_convert_fusion
  282.8 6.9 fusion.183
  289.8 6.9 fusion.184
  296.7 4.4 convolution_convert_fusion.1
  301.1 4.5 fusion.76
  305.7 3.7 multiply_reduce_fusion.2
  315.3 17.4 %shard_map.338 = (bf16[1024,768]{1,0:T(8,128)(2,1)}, bf16[1024,768]{1,0:T(8,128)(2,1)}, bf16[1024,768]{1,0:T(8,128)(2,1)}, f32[16,768]{1,0:T(8,128)}) custom-call(s32[2]{0:T(128)} %lengths.2, bf16[1024,1536]{1,0:T(8,128)(2,1)} %add_convert_fusion.q_ref.k_ref, bf16[1024,1536]{1,0:T(8,128)(2,1)} %add_convert_fusion.q_ref.k_ref, ...), custom_call_target="tpu_custom_call" | custom-call | tf_op jit(solution)/shard_map/pallas_call | solution.py:196
  332.7 17.4 %shard_map.339 = (bf16[1024,768]{1,0:T(8,128)(2,1)}, bf16[1024,768]{1,0:T(8,128)(2,1)}, bf16[1024,768]{1,0:T(8,128)(2,1)}, f32[16,768]{1,0:T(8,128)}) custom-call(s32[2]{0:T(128)} %lengths.2, bf16[1024,1536]{1,0:T(8,128)(2,1)} %add_convert_fusion.q_ref.k_ref, ...), custom_call_target="tpu_custom_call", output_to_operand_aliasing={{0}: (5, {}), {1}: (6, {}), {2}: (7, {}), {3}: (8, {})} | custom-call | tf_op jit(solution)/shard_map/pallas_call | solution.py:196
  413.8 4.4 multiply_subtract_fusion
  420.3 4.4 all-to-all-start.3
  444.0 9.0 %collective-permute-done.27 = bf16[4,48,384]{2,1,0:T(8,128)(2,1)S(1)} collective-permute-done((bf16[4,48,384]{2,1,0:T(8,128)(2,1)S(1)}, bf16[4,48,384]{2,1,0:T(8,128)(2,1)S(1)}, u32[]{:S(2)}, u32[]{:S(2)}) %collective-permute-start.27) | collective-permute-done | bytes 147488 | tf_op jit(solution)/shard_map/ppermute | solution.py:60
  454.7 7.5 %collective-permute-done.32 = bf16[4,48,384]{2,1,0:T(8,128)(2,1)S(1)} collective-permute-done((bf16[4,48,384]{2,1,0:T(8,128)(2,1)S(1)}, bf16[4,48,384]{2,1,0:T(8,128)(2,1)S(1)}, u32[]{:S(2)}, u32[]{:S(2)}) %collective-permute-start.32) | collective-permute-done | bytes 147488 | tf_op jit(solution)/shard_map/ppermute | solution.py:60
  475.4 4.5 collective-permute-done.23
  481.2 4.4 collective-permute-done.24
  489.3 4.5 convert_add_fusion.1
  495.2 4.3 convert_add_fusion
  501.2 20.7 %collective-permute-done.42 = bf16[384,1536]{1,0:T(8,128)(2,1)S(1)} collective-permute-done((bf16[384,1536]{1,0:T(8,128)(2,1)S(1)}, bf16[384,1536]{1,0:T(8,128)(2,1)S(1)}, u32[]{:S(2)}, u32[]{:S(2)}) %collective-permute-start.42) | collective-permute-done | bytes 1179680 | tf_op jit(solution)/shard_map/ppermute | solution.py:60
  530.6 6.6 multiply_reduce_fusion.5
  545.6 4.0 all-to-all-start.4
  549.6 6.8 collective-permute-done.43
  562.1 4.7 collective-permute-done.44
  570.1 8.9 %collective-permute-done.45 = bf16[48,1536]{1,0:T(8,128)(2,1)S(1)} collective-permute-done((bf16[48,1536]{1,0:T(8,128)(2,1)S(1)}, bf16[48,1536]{1,0:T(8,128)(2,1)S(1)}, u32[]{:S(2)}, u32[]{:S(2)}) %collective-permute-start.45) | collective-permute-done | bytes 147488 | tf_op jit(solution)/shard_map/ppermute | solution.py:60
  598.5 4.3 all-to-all-start.5
  611.8 30.0 %table_update.1 = (f32[15632,384]{1,0:T(8,128)}, bf16[15632,384]{1,0:T(8,128)(2,1)}) custom-call(s32[2048]{0:T(1024)} %copy-done.52, s32[9]{0:T(128)} %convert_reduce_fusion.1.starts, f32[15632,384]{1,0:T(8,128)} %table_ref.3, f32[2048,384]{1,0:T(8,128)} %get-tuple-element.241.update_ref, f32[1,384]{1,0:T(1,128)} %broadcast_in_dim.82.scale_ref), custom_call_target="tpu_custom_call" | custom-call | tf_op jit(solution)/shard_map/table_update/pallas_call | solution.py:256
  645.5 6.8 all-to-all-start.6
  653.8 4.0 concatenate.689
  671.7 11.2 %all-to-all-done.6 = f32[16,56,384]{2,1,0:T(8,128)} async-done(((f32[16,56,384]{2,1,0:T(8,128)}), f32[16,56,384]{2,1,0:T(8,128)}, u32[]{:S(2)}, u32[]{:S(2)}) %all-to-all-start.6) | async-done | bytes 1376288 | tf_op jit(solution)/shard_map/all_to_all | solution.py:118
  (606 shorter events, 258.9 us)
Async XLA Ops:
  3.1 27.2 %all-to-all-start = ((s32[16,1,64]{2,1,0:T(1,128)}), s32[16,1,64]{2,1,0:T(1,128)S(1)}, u32[]{:S(2)}, u32[]{:S(2)}) async-start(s32[16,1,64]{2,1,0:T(1,128)} %all_to_all.26), calls=%async_computation | async-start | bytes 16384 | tf_op jit(solution)/shard_map/all_to_all | solution.py:413
  12.7 47.8 %collective-permute-start.7 = (bf16[1,1,1,1,48,1536]{5,4,0,3,2,1:T(8,128)(2,1)S(1)}, bf16[1,1,1,1,48,1536]{5,4,0,3,2,1:T(8,128)(2,1)S(1)}, u32[]{:S(2)}, u32[]{:S(2)}) collective-permute-start(bf16[1,1,1,1,48,1536]{5,4,0,3,2,1:T(8,128)(2,1)S(1)} %get-tuple-element.264), channel_id=1, source_target_pairs={{0,16},{2,18},{4,20},{6,22},{8,24},{10,26},{12,28},{14,30},{16,0},... | collective-permute-start | bytes 442376 | tf_op jit(solution)/shard_map/ppermute | solution.py:60
  15.6 47.0 %collective-permute-start.2 = (bf16[1,1,1,1,48,1536]{5,4,3,2,1,0:T(8,128)(2,1)S(1)}, bf16[1,1,1,1,48,1536]{5,4,3,2,1,0:T(8,128)(2,1)S(1)}, u32[]{:S(2)}, u32[]{:S(2)}) collective-permute-start(bf16[1,1,1,1,48,1536]{5,4,3,2,1,0:T(8,128)(2,1)S(1)} %get-tuple-element.263), channel_id=1, source_target_pairs={{0,16},{2,18},{4,20},{6,22},{8,24},{10,26},{12,28},{14,30},{16,0},... | collective-permute-start | bytes 442376 | tf_op jit(solution)/shard_map/ppermute | solution.py:60
  15.7 48.5 %collective-permute-start.12 = (bf16[1,1,1,1,48,1536]{5,4,3,2,1,0:T(8,128)(2,1)S(1)}, bf16[1,1,1,1,48,1536]{5,4,3,2,1,0:T(8,128)(2,1)S(1)}, u32[]{:S(2)}, u32[]{:S(2)}) collective-permute-start(bf16[1,1,1,1,48,1536]{5,4,3,2,1,0:T(8,128)(2,1)S(1)} %get-tuple-element.262), channel_id=1, source_target_pairs={{0,16},{2,18},{4,20},{6,22},{8,24},{10,26},{12,28},{14,30},{16,0},... | collective-permute-start | bytes 442376 | tf_op jit(solution)/shard_map/ppermute | solution.py:60
  53.6 97.8 %all-to-all-start.1 = ((bf16[16,2,64,384]{3,2,1,0:T(8,128)(2,1)}), bf16[16,2,64,384]{3,2,1,0:T(8,128)(2,1)S(1)}, u32[]{:S(2)}, u32[]{:S(2)}) async-start(bf16[16,2,64,384]{3,2,1,0:T(8,128)(2,1)} %bitcast.400), calls=%async_computation.1 | async-start | bytes 3145728 | tf_op jit(solution)/shard_map/all_to_all | solution.py:440
  60.5 12.3 %collective-permute-start.8 = (bf16[2,1,1,1,48,1536]{5,4,0,3,2,1:T(8,128)(2,1)S(1)}, bf16[2,1,1,1,48,1536]{5,4,0,3,2,1:T(8,128)(2,1)S(1)}, u32[]{:S(2)}, u32[]{:S(2)}) collective-permute-start(bf16[2,1,1,1,48,1536]{5,4,0,3,2,1:T(8,128)(2,1)S(1)} %maximum_select_fusion.13), channel_id=1, source_target_pairs={{0,2},{2,0},{4,6},{6,4},{8,10},{10,8},{12,14},{14,12},{16,18},{18,... | collective-permute-start | bytes 884744 | tf_op jit(solution)/shard_map/ppermute | solution.py:60
  62.6 45.8 %collective-permute-start.3 = (bf16[2,1,1,1,48,1536]{5,4,3,2,1,0:T(8,128)(2,1)S(1)}, bf16[2,1,1,1,48,1536]{5,4,3,2,1,0:T(8,128)(2,1)S(1)}, u32[]{:S(2)}, u32[]{:S(2)}) collective-permute-start(bf16[2,1,1,1,48,1536]{5,4,3,2,1,0:T(8,128)(2,1)S(1)} %bitcast_select_fusion.1), channel_id=1, source_target_pairs={{0,8},{2,10},{4,12},{6,14},{8,0},{10,2},{12,4},{14,6},{16,24},{18,... | collective-permute-start | bytes 884744 | tf_op jit(solution)/shard_map/ppermute | solution.py:60
  64.2 44.4 %collective-permute-start.13 = (bf16[2,1,1,1,48,1536]{5,4,3,2,1,0:T(8,128)(2,1)S(1)}, bf16[2,1,1,1,48,1536]{5,4,3,2,1,0:T(8,128)(2,1)S(1)}, u32[]{:S(2)}, u32[]{:S(2)}) collective-permute-start(bf16[2,1,1,1,48,1536]{5,4,3,2,1,0:T(8,128)(2,1)S(1)} %bitcast_select_fusion), channel_id=1, source_target_pairs={{0,4},{2,6},{4,0},{6,2},{8,12},{10,14},{12,8},{14,10},{16,20},{18,... | collective-permute-start | bytes 884744 | tf_op jit(solution)/shard_map/ppermute | solution.py:60
  72.9 32.9 %collective-permute-start.9 = (bf16[2,1,1,2,48,1536]{5,4,0,3,2,1:T(8,128)(2,1)S(1)}, bf16[2,1,1,2,48,1536]{5,4,0,3,2,1:T(8,128)(2,1)S(1)}, u32[]{:S(2)}, u32[]{:S(2)}) collective-permute-start(bf16[2,1,1,2,48,1536]{5,4,0,3,2,1:T(8,128)(2,1)S(1)} %maximum_select_fusion.9), channel_id=1, source_target_pairs={{0,8},{2,10},{4,12},{6,14},{8,0},{10,2},{12,4},{14,6},{16,24},{18,... | collective-permute-start | bytes 1769480 | tf_op jit(solution)/shard_map/ppermute | solution.py:60
  106.0 41.6 %collective-permute-start.10 = (bf16[2,2,1,2,48,1536]{5,4,0,3,2,1:T(8,128)(2,1)S(1)}, bf16[2,2,1,2,48,1536]{5,4,0,3,2,1:T(8,128)(2,1)S(1)}, u32[]{:S(2)}, u32[]{:S(2)}) collective-permute-start(bf16[2,2,1,2,48,1536]{5,4,0,3,2,1:T(8,128)(2,1)S(1)} %maximum_select_fusion.4), channel_id=1, source_target_pairs={{0,4},{2,6},{4,0},{6,2},{8,12},{10,14},{12,8},{14,10},{16,20},{18,... | collective-permute-start | bytes 3538952 | tf_op jit(solution)/shard_map/ppermute | solution.py:60
  108.5 38.1 %collective-permute-start.4 = (bf16[2,2,1,1,48,1536]{5,4,3,2,1,0:T(8,128)(2,1)S(1)}, bf16[2,2,1,1,48,1536]{5,4,3,2,1,0:T(8,128)(2,1)S(1)}, u32[]{:S(2)}, u32[]{:S(2)}) collective-permute-start(bf16[2,2,1,1,48,1536]{5,4,3,2,1,0:T(8,128)(2,1)S(1)} %maximum_select_fusion.7), channel_id=1, source_target_pairs={{0,4},{2,6},{4,0},{6,2},{8,12},{10,14},{12,8},{14,10},{16,20},{18,... | collective-permute-start | bytes 1769480 | tf_op jit(solution)/shard_map/ppermute | solution.py:60
  108.8 40.8 %collective-permute-start.14 = (bf16[2,1,2,1,48,1536]{5,4,3,2,1,0:T(8,128)(2,1)S(1)}, bf16[2,1,2,1,48,1536]{5,4,3,2,1,0:T(8,128)(2,1)S(1)}, u32[]{:S(2)}, u32[]{:S(2)}) collective-permute-start(bf16[2,1,2,1,48,1536]{5,4,3,2,1,0:T(8,128)(2,1)S(1)} %maximum_select_fusion.11), channel_id=1, source_target_pairs={{0,2},{2,0},{4,6},{6,4},{8,10},{10,8},{12,14},{14,12},{16,18},{18,... | collective-permute-start | bytes 1769480 | tf_op jit(solution)/shard_map/ppermute | solution.py:60
  146.7 26.8 %collective-permute-start.5 = (bf16[2,2,2,1,48,1536]{5,4,3,2,1,0:T(8,128)(2,1)S(1)}, bf16[2,2,2,1,48,1536]{5,4,3,2,1,0:T(8,128)(2,1)}, u32[]{:S(2)}, u32[]{:S(2)}) collective-permute-start(bf16[2,2,2,1,48,1536]{5,4,3,2,1,0:T(8,128)(2,1)S(1)} %maximum_select_fusion.3), channel_id=1, source_target_pairs={{0,2},{2,0},{4,6},{6,4},{8,10},{10,8},{12,14},{14,12},{16,18},{18,... | collective-permute-start | bytes 3538952 | tf_op jit(solution)/shard_map/ppermute | solution.py:60
  149.6 39.3 %collective-permute-start.11 = (bf16[768,1536]{1,0:T(8,128)(2,1)}, bf16[768,1536]{1,0:T(8,128)(2,1)}, u32[]{:S(2)}, u32[]{:S(2)}) collective-permute-start(bf16[768,1536]{1,0:T(8,128)(2,1)} %bitcast.26), channel_id=1, source_target_pairs={{0,1},{1,0},{2,3},{3,2},{4,5},{5,4},{6,7},{7,6},{8,9},{9,8},{10,11... | collective-permute-start | bytes 7077896 | tf_op jit(solution)/shard_map/ppermute | solution.py:60
  150.7 28.7 %collective-permute-start.15 = (bf16[2,1,2,2,48,1536]{5,4,3,2,1,0:T(8,128)(2,1)}, bf16[2,1,2,2,48,1536]{5,4,3,2,1,0:T(8,128)(2,1)}, u32[]{:S(2)}, u32[]{:S(2)}) collective-permute-start(bf16[2,1,2,2,48,1536]{5,4,3,2,1,0:T(8,128)(2,1)} %maximum_select_fusion.5), channel_id=1, source_target_pairs={{0,8},{2,10},{4,12},{6,14},{8,0},{10,2},{12,4},{14,6},{16,24},{18,... | collective-permute-start | bytes 3538952 | tf_op jit(solution)/shard_map/ppermute | solution.py:60
  151.7 32.2 %collective-permute-start.1 = (bf16[1024,384]{1,0:T(8,128)(2,1)S(1)}, bf16[1024,384]{1,0:T(8,128)(2,1)S(1)}, u32[]{:S(2)}, u32[]{:S(2)}) collective-permute-start(bf16[1024,384]{1,0:T(8,128)(2,1)S(1)} %bitcast.448), channel_id=1, source_target_pairs={{0,1},{1,0},{2,3},{3,2},{4,5},{5,4},{6,7},{7,6},{8,9},{9,8},{10,11... | collective-permute-start | bytes 2359304 | tf_op jit(solution)/shard_map/ppermute | solution.py:60
  175.5 19.5 %collective-permute-start.6 = (bf16[768,1536]{1,0:T(8,128)(2,1)S(1)}, bf16[768,1536]{1,0:T(8,128)(2,1)S(1)}, u32[]{:S(2)}, u32[]{:S(2)}) collective-permute-start(bf16[768,1536]{1,0:T(8,128)(2,1)S(1)} %bitcast.391), channel_id=1, source_target_pairs={{0,1},{1,0},{2,3},{3,2},{4,5},{5,4},{6,7},{7,6},{8,9},{9,8},{10,11... | collective-permute-start | bytes 7077896 | tf_op jit(solution)/shard_map/ppermute | solution.py:60
  183.8 46.5 %collective-permute-start.16 = (bf16[768,1536]{1,0:T(8,128)(2,1)}, bf16[768,1536]{1,0:T(8,128)(2,1)}, u32[]{:S(2)}, u32[]{:S(2)}) collective-permute-start(bf16[768,1536]{1,0:T(8,128)(2,1)} %bitcast.37), channel_id=1, source_target_pairs={{0,1},{1,0},{2,3},{3,2},{4,5},{5,4},{6,7},{7,6},{8,9},{9,8},{10,11... | collective-permute-start | bytes 7077896 | tf_op jit(solution)/shard_map/ppermute | solution.py:60
  249.9 13.9 %all-to-all-start.2 = ((f32[32,2,768]{2,1,0:T(2,128)}), f32[32,2,768]{2,1,0:T(2,128)S(1)}, u32[]{:S(2)}, u32[]{:S(2)}) async-start(f32[32,2,768]{2,1,0:T(2,128)} %broadcast_in_dim.77), calls=%async_computation.2 | async-start | bytes 393216 | tf_op jit(solution)/shard_map/all_to_all | solution.py:118
  368.8 27.1 %collective-permute-start.17 = (bf16[1024,384]{1,0:T(8,128)(2,1)}, bf16[1024,384]{1,0:T(8,128)(2,1)}, u32[]{:S(2)}, u32[]{:S(2)}) collective-permute-start(bf16[1024,384]{1,0:T(8,128)(2,1)} %get-tuple-element.251), channel_id=1, source_target_pairs={{0,1},{1,0},{2,3},{3,2},{4,5},{5,4},{6,7},{7,6},{8,9},{9,8},{10,11... | collective-permute-start | bytes 2359304 | tf_op jit(solution)/shard_map/ppermute | solution.py:60
  369.5 11.9 %collective-permute-start.36 = (bf16[768,384]{1,0:T(8,128)(2,1)}, bf16[768,384]{1,0:T(8,128)(2,1)}, u32[]{:S(2)}, u32[]{:S(2)}) collective-permute-start(bf16[768,384]{1,0:T(8,128)(2,1)} %convolution_convert_fusion.3), channel_id=1, source_target_pairs={{0,1},{1,0},{2,3},{3,2},{4,5},{5,4},{6,7},{7,6},{8,9},{9,8},{10,11... | collective-permute-start | bytes 1769480 | tf_op jit(solution)/shard_map/ppermute | solution.py:60
  369.5 119.7 %collective-permute-start.41 = (bf16[768,1536]{1,0:T(8,128)(2,1)}, bf16[768,1536]{1,0:T(8,128)(2,1)}, u32[]{:S(2)}, u32[]{:S(2)}) collective-permute-start(bf16[768,1536]{1,0:T(8,128)(2,1)} %convolution_convert_fusion.1), channel_id=1, source_target_pairs={{0,1},{1,0},{2,3},{3,2},{4,5},{5,4},{6,7},{7,6},{8,9},{9,8},{10,11... | collective-permute-start | bytes 7077896 | tf_op jit(solution)/shard_map/ppermute | solution.py:60
  370.0 15.0 %collective-permute-start.30 = (bf16[768,384]{1,0:T(8,128)(2,1)}, bf16[768,384]{1,0:T(8,128)(2,1)}, u32[]{:S(2)}, u32[]{:S(2)}) collective-permute-start(bf16[768,384]{1,0:T(8,128)(2,1)} %convolution_convert_fusion.4), channel_id=1, source_target_pairs={{0,1},{1,0},{2,3},{3,2},{4,5},{5,4},{6,7},{7,6},{8,9},{9,8},{10,11... | collective-permute-start | bytes 1769480 | tf_op jit(solution)/shard_map/ppermute | solution.py:60
  372.7 8.5 %collective-permute-start.20 = (bf16[512,384]{1,0:T(8,128)(2,1)S(1)}, bf16[512,384]{1,0:T(8,128)(2,1)S(1)}, u32[]{:S(2)}, u32[]{:S(2)}) collective-permute-start(bf16[512,384]{1,0:T(8,128)(2,1)S(1)} %dynamic-slice_convert_fusion.4), channel_id=1, source_target_pairs={{0,1},{1,0},{2,3},{3,2},{4,5},{5,4},{6,7},{7,6},{8,9},{9,8},{10,11... | collective-permute-start | bytes 1179656 | tf_op jit(solution)/shard_map/ppermute | solution.py:60
  381.2 114.0 %collective-permute-start.46 = (bf16[768,1536]{1,0:T(8,128)(2,1)}, bf16[768,1536]{1,0:T(8,128)(2,1)}, u32[]{:S(2)}, u32[]{:S(2)}) collective-permute-start(bf16[768,1536]{1,0:T(8,128)(2,1)} %convolution_convert_fusion), channel_id=1, source_target_pairs={{0,1},{1,0},{2,3},{3,2},{4,5},{5,4},{6,7},{7,6},{8,9},{9,8},{10,11... | collective-permute-start | bytes 7077896 | tf_op jit(solution)/shard_map/ppermute | solution.py:60
  381.4 6.8 collective-permute-start.25
  388.2 44.8 %collective-permute-start.37 = (bf16[384,384]{1,0:T(8,128)(2,1)}, bf16[384,384]{1,0:T(8,128)(2,1)}, u32[]{:S(2)}, u32[]{:S(2)}) collective-permute-start(bf16[384,384]{1,0:T(8,128)(2,1)} %bitcast.85), channel_id=1, source_target_pairs={{0,8},{2,10},{4,12},{6,14},{8,0},{10,2},{12,4},{14,6},{16,24},{18,... | collective-permute-start | bytes 884744 | tf_op jit(solution)/shard_map/ppermute | solution.py:60
  390.7 45.2 %collective-permute-start.26 = (bf16[8,48,384]{2,1,0:T(8,128)(2,1)}, bf16[8,48,384]{2,1,0:T(8,128)(2,1)}, u32[]{:S(2)}, u32[]{:S(2)}) collective-permute-start(bf16[8,48,384]{2,1,0:T(8,128)(2,1)} %bitcast.65), channel_id=1, source_target_pairs={{0,4},{2,6},{4,0},{6,2},{8,12},{10,14},{12,8},{14,10},{16,20},{18,... | collective-permute-start | bytes 884744 | tf_op jit(solution)/shard_map/ppermute | solution.py:60
  395.9 42.7 %collective-permute-start.31 = (bf16[8,48,384]{2,1,0:T(8,128)(2,1)S(1)}, bf16[8,48,384]{2,1,0:T(8,128)(2,1)}, u32[]{:S(2)}, u32[]{:S(2)}) collective-permute-start(bf16[8,48,384]{2,1,0:T(8,128)(2,1)S(1)} %bitcast.462), channel_id=1, source_target_pairs={{0,8},{2,10},{4,12},{6,14},{8,0},{10,2},{12,4},{14,6},{16,24},{18,... | collective-permute-start | bytes 884744 | tf_op jit(solution)/shard_map/ppermute | solution.py:60
  420.3 110.3 %all-to-all-start.3 = ((bf16[16,2,64,384]{3,2,1,0:T(8,128)(2,1)}), bf16[16,2,64,384]{3,2,1,0:T(8,128)(2,1)}, u32[]{:S(2)}, u32[]{:S(2)}) async-start(bf16[16,2,64,384]{3,2,1,0:T(8,128)(2,1)} %pad_maximum_fusion), calls=%async_computation.3 | async-start | bytes 3145728 | tf_op jit(solution)/shard_map/all_to_all | solution.py:569
  432.9 30.8 %collective-permute-start.21 = (bf16[8,80,384]{2,1,0:T(8,128)(2,1)}, bf16[8,80,384]{2,1,0:T(8,128)(2,1)S(1)}, u32[]{:S(2)}, u32[]{:S(2)}) collective-permute-start(bf16[8,80,384]{2,1,0:T(8,128)(2,1)} %fusion.110), channel_id=1, source_target_pairs={{0,2},{2,0},{4,6},{6,4},{8,10},{10,8},{12,14},{14,12},{16,18},{18,... | collective-permute-start | bytes 1474568 | tf_op jit(solution)/shard_map/ppermute | solution.py:60
  435.9 7.3 %collective-permute-start.38 = (bf16[192,384]{1,0:T(8,128)(2,1)S(1)}, bf16[192,384]{1,0:T(8,128)(2,1)S(1)}, u32[]{:S(2)}, u32[]{:S(2)}) collective-permute-start(bf16[192,384]{1,0:T(8,128)(2,1)S(1)} %bitcast.466), channel_id=1, source_target_pairs={{0,4},{2,6},{4,0},{6,2},{8,12},{10,14},{12,8},{14,10},{16,20},{18,... | collective-permute-start | bytes 442376 | tf_op jit(solution)/shard_map/ppermute | solution.py:60
  438.6 14.4 %collective-permute-start.27 = (bf16[4,48,384]{2,1,0:T(8,128)(2,1)S(1)}, bf16[4,48,384]{2,1,0:T(8,128)(2,1)S(1)}, u32[]{:S(2)}, u32[]{:S(2)}) collective-permute-start(bf16[4,48,384]{2,1,0:T(8,128)(2,1)S(1)} %bitcast.467), channel_id=1, source_target_pairs={{0,8},{2,10},{4,12},{6,14},{8,0},{10,2},{12,4},{14,6},{16,24},{18,... | collective-permute-start | bytes 442376 | tf_op jit(solution)/shard_map/ppermute | solution.py:60
  443.2 18.9 %collective-permute-start.32 = (bf16[4,48,384]{2,1,0:T(8,128)(2,1)S(1)}, bf16[4,48,384]{2,1,0:T(8,128)(2,1)S(1)}, u32[]{:S(2)}, u32[]{:S(2)}) collective-permute-start(bf16[4,48,384]{2,1,0:T(8,128)(2,1)S(1)} %fusion.114), channel_id=1, source_target_pairs={{0,2},{2,0},{4,6},{6,4},{8,10},{10,8},{12,14},{14,12},{16,18},{18,... | collective-permute-start | bytes 442376 | tf_op jit(solution)/shard_map/ppermute | solution.py:60
  453.0 11.9 %collective-permute-start.39 = (bf16[96,384]{1,0:T(8,128)(2,1)S(1)}, bf16[96,384]{1,0:T(8,128)(2,1)S(1)}, u32[]{:S(2)}, u32[]{:S(2)}) collective-permute-start(bf16[96,384]{1,0:T(8,128)(2,1)S(1)} %bitcast.470), channel_id=1, source_target_pairs={{0,2},{2,0},{4,6},{6,4},{8,10},{10,8},{12,14},{14,12},{16,18},{18,... | collective-permute-start | bytes 221192 | tf_op jit(solution)/shard_map/ppermute | solution.py:60
  466.5 19.2 %collective-permute-start.40 = (bf16[48,384]{1,0:T(8,128)(2,1)S(1)}, bf16[48,384]{1,0:T(8,128)(2,1)S(1)}, u32[]{:S(2)}, u32[]{:S(2)}) collective-permute-start(bf16[48,384]{1,0:T(8,128)(2,1)S(1)} %fusion.128), channel_id=1, source_target_pairs={{0,16},{2,18},{4,20},{6,22},{8,24},{10,26},{12,28},{14,30},{16,0},... | collective-permute-start | bytes 110600 | tf_op jit(solution)/shard_map/ppermute | solution.py:60
  471.2 10.0 %collective-permute-start.34 = (bf16[1,48,384]{2,1,0:T(8,128)(2,1)S(1)}, bf16[1,48,384]{2,1,0:T(8,128)(2,1)S(1)}, u32[]{:S(2)}, u32[]{:S(2)}) collective-permute-start(bf16[1,48,384]{2,1,0:T(8,128)(2,1)S(1)} %dynamic-slice_convert_fusion.20), channel_id=1, source_target_pairs={{0,16},{2,18},{4,20},{6,22},{8,24},{10,26},{12,28},{14,30},{16,0},... | collective-permute-start | bytes 110600 | tf_op jit(solution)/shard_map/ppermute | solution.py:60
  493.9 28.1 %collective-permute-start.42 = (bf16[384,1536]{1,0:T(8,128)(2,1)S(1)}, bf16[384,1536]{1,0:T(8,128)(2,1)S(1)}, u32[]{:S(2)}, u32[]{:S(2)}) collective-permute-start(bf16[384,1536]{1,0:T(8,128)(2,1)S(1)} %bitcast.436), channel_id=1, source_target_pairs={{0,4},{2,6},{4,0},{6,2},{8,12},{10,14},{12,8},{14,10},{16,20},{18,... | collective-permute-start | bytes 3538952 | tf_op jit(solution)/shard_map/ppermute | solution.py:60
  499.7 28.0 %collective-permute-start.47 = (bf16[384,1536]{1,0:T(8,128)(2,1)S(1)}, bf16[384,1536]{1,0:T(8,128)(2,1)S(1)}, u32[]{:S(2)}, u32[]{:S(2)}) collective-permute-start(bf16[384,1536]{1,0:T(8,128)(2,1)S(1)} %bitcast.437), channel_id=1, source_target_pairs={{0,2},{2,0},{4,6},{6,4},{8,10},{10,8},{12,14},{14,12},{16,18},{18,... | collective-permute-start | bytes 3538952 | tf_op jit(solution)/shard_map/ppermute | solution.py:60
  539.5 16.9 %collective-permute-start.43 = (bf16[192,1536]{1,0:T(8,128)(2,1)}, bf16[192,1536]{1,0:T(8,128)(2,1)}, u32[]{:S(2)}, u32[]{:S(2)}) collective-permute-start(bf16[192,1536]{1,0:T(8,128)(2,1)} %bitcast.100), channel_id=1, source_target_pairs={{0,2},{2,0},{4,6},{6,4},{8,10},{10,8},{12,14},{14,12},{16,18},{18,... | collective-permute-start | bytes 1769480 | tf_op jit(solution)/shard_map/ppermute | solution.py:60
  540.6 18.9 %collective-permute-start.48 = (bf16[192,1536]{1,0:T(8,128)(2,1)}, bf16[192,1536]{1,0:T(8,128)(2,1)}, u32[]{:S(2)}, u32[]{:S(2)}) collective-permute-start(bf16[192,1536]{1,0:T(8,128)(2,1)} %bitcast.112), channel_id=1, source_target_pairs={{0,8},{2,10},{4,12},{6,14},{8,0},{10,2},{12,4},{14,6},{16,24},{18,... | collective-permute-start | bytes 1769480 | tf_op jit(solution)/shard_map/ppermute | solution.py:60
  545.6 40.3 %all-to-all-start.4 = ((f32[32,16,128]{2,1,0:T(8,128)}), f32[32,16,128]{2,1,0:T(8,128)S(1)}, u32[]{:S(2)}, u32[]{:S(2)}) async-start(f32[32,16,128]{2,1,0:T(8,128)} %bitcast.183), calls=%async_computation.4 | async-start | bytes 524288 | tf_op jit(solution)/shard_map/all_to_all | solution.py:656
  558.0 8.8 %collective-permute-start.44 = (bf16[96,1536]{1,0:T(8,128)(2,1)S(1)}, bf16[96,1536]{1,0:T(8,128)(2,1)S(1)}, u32[]{:S(2)}, u32[]{:S(2)}) collective-permute-start(bf16[96,1536]{1,0:T(8,128)(2,1)S(1)} %bitcast.463), channel_id=1, source_target_pairs={{0,8},{2,10},{4,12},{6,14},{8,0},{10,2},{12,4},{14,6},{16,24},{18,... | collective-permute-start | bytes 884744 | tf_op jit(solution)/shard_map/ppermute | solution.py:60
  560.9 7.1 %collective-permute-start.49 = (bf16[96,1536]{1,0:T(8,128)(2,1)S(1)}, bf16[96,1536]{1,0:T(8,128)(2,1)S(1)}, u32[]{:S(2)}, u32[]{:S(2)}) collective-permute-start(bf16[96,1536]{1,0:T(8,128)(2,1)S(1)} %bitcast.464), channel_id=1, source_target_pairs={{0,4},{2,6},{4,0},{6,2},{8,12},{10,14},{12,8},{14,10},{16,20},{18,... | collective-permute-start | bytes 884744 | tf_op jit(solution)/shard_map/ppermute | solution.py:60
  566.9 12.1 %collective-permute-start.45 = (bf16[48,1536]{1,0:T(8,128)(2,1)S(1)}, bf16[48,1536]{1,0:T(8,128)(2,1)S(1)}, u32[]{:S(2)}, u32[]{:S(2)}) collective-permute-start(bf16[48,1536]{1,0:T(8,128)(2,1)S(1)} %fusion.115), channel_id=1, source_target_pairs={{0,16},{2,18},{4,20},{6,22},{8,24},{10,26},{12,28},{14,30},{16,0},... | collective-permute-start | bytes 442376 | tf_op jit(solution)/shard_map/ppermute | solution.py:60
  568.1 14.0 %collective-permute-start.50 = (bf16[48,1536]{1,0:T(8,128)(2,1)S(1)}, bf16[48,1536]{1,0:T(8,128)(2,1)S(1)}, u32[]{:S(2)}, u32[]{:S(2)}) collective-permute-start(bf16[48,1536]{1,0:T(8,128)(2,1)S(1)} %fusion.116), channel_id=1, source_target_pairs={{0,16},{2,18},{4,20},{6,22},{8,24},{10,26},{12,28},{14,30},{16,0},... | collective-permute-start | bytes 442376 | tf_op jit(solution)/shard_map/ppermute | solution.py:60
  598.5 43.4 %all-to-all-start.5 = ((f32[16,80,128]{2,1,0:T(8,128)}), f32[16,80,128]{2,1,0:T(8,128)}, u32[]{:S(2)}, u32[]{:S(2)}) async-start(f32[16,80,128]{2,1,0:T(8,128)} %broadcast_in_dim.96), calls=%async_computation.5 | async-start | bytes 1310720 | tf_op jit(solution)/shard_map/all_to_all | solution.py:118
  645.5 37.5 %all-to-all-start.6 = ((f32[16,56,384]{2,1,0:T(8,128)}), f32[16,56,384]{2,1,0:T(8,128)}, u32[]{:S(2)}, u32[]{:S(2)}) async-start(f32[16,56,384]{2,1,0:T(8,128)} %broadcast_in_dim.97), calls=%async_computation.6 | async-start | bytes 2752512 | tf_op jit(solution)/shard_map/all_to_all | solution.py:118
  (111 other events, 1356.1 us)
where the time goes:
time: 717 us; the launch traced here: 708 us
  waiting for transfers between devices  198 us (28%)
  matrix products  116 us (16%)
  other arithmetic  109 us (15%)
  Pallas kernels  103 us (14%)
  starting transfers between devices  88.8 us (12%)
  local copies, waits for them, and re-layouts  76.5 us (11%)
  between operations  16.9 us (2%)
    ppermute x55, waiting for transfers between devices, swap_by(): return lax.ppermute(values, axis, [(i, i ^ mask) for i in range(size)])  180 us
    dot_general x31, matrix products, dot(): return lax.dot_general(left, right, dims, preferred_element_type=F32)  110 us
    ppermute x55, starting transfers between devices, swap_by(): return lax.ppermute(values, axis, [(i, i ^ mask) for i in range(size)])  51.1 us
    pallas_call x2, Pallas kernels, attend_back(): pl.pallas_call(functools.partial(attention_back_kernel, seq), grid_spec=p...  34.8 us
    pallas_call x1, Pallas kernels, table_update(): pl.pallas_call(table_kernel, grid_spec=pltpu.PrefetchScalarGridSpec(num_s...  30 us
    unnamed x233, local copies, waits for them, and re-layouts  28.2 us
    all_to_all x3, waiting for transfers between devices, everyone(): lax.all_to_all(jnp.broadcast_to(values[None], (size,) + values.shape), ax...  18.1 us
    all_to_all x3, starting transfers between devices, everyone(): lax.all_to_all(jnp.broadcast_to(values[None], (size,) + values.shape), ax...  16.1 us
  transfers between devices with their start and end apart: 62, of which 24 were waited for; matrix products, arithmetic and copies ran while one was open for 24% of the time, Pallas kernels for 9%

commit v1 on v0

--- a/solution.py
+++ b/solution.py
@@ -359,10 +359,10 @@
     return (gradient * lax.rsqrt(moment_new), moment_new)
 
 
-def apply_update(weight_matrix, update):
+def apply_update(weight_matrix, update, square):
     spread = jnp.sqrt(jnp.mean(update * update))
     clip_factor = jnp.maximum(1.0, spread / CLIP_LIMIT)
-    step_size = RELATIVE * jnp.maximum(FLOOR_SCALE, jnp.sqrt(jnp.mean(weight_matrix * weight_matrix)))
+    step_size = RELATIVE * jnp.maximum(FLOOR_SCALE, jnp.sqrt(square))
     return (weight_matrix - step_size * (update / clip_factor), spread)
 
 
@@ -437,7 +437,10 @@
     w_v, w_o = w_vo[:, :MODEL_WIDTH], w_vo[:, MODEL_WIDTH:]
 
     looked = take_rows(wanted, embedding).reshape(outer, inner, cap, shard_cols)
+    looked, *early = lax.optimization_barrier((looked, head_weight, positions, norm_vectors, layers[0]))
     replies = lax.all_to_all(looked, "dp", 0, 0, tiled=True)
+    head_square, pos_square, vector_square = (jnp.mean(weight * weight) for weight in early[:3])
+    layer_column_squares = jnp.sum(early[3] * early[3], 0)
     own_part = replies[:, 0].reshape(slots, shard_cols)
     other_parts = [swap_by(replies[:, d].reshape(slots, shard_cols), "fsdp", inner, d) for d in range(1, inner)]
     rows_low = in_order([own_part] + other_parts, inner, 1)
@@ -531,6 +534,10 @@
     back = jnp.concatenate([rows.reshape(outer, 1, cap, shard_cols) for rows in parts], 1)
     (
         back,
+        d_embedded,
+        d_q,
+        d_k,
+        d_v,
         embed_rows,
         embed_cols,
         layer_rows,
@@ -549,6 +556,10 @@
     ) = lax.optimization_barrier(
         (
             back,
+            d_embedded,
+            d_q,
+            d_k,
+            d_v,
             embed_rows,
             embed_cols,
             layer_rows,
@@ -568,6 +579,9 @@
     )
     returned = lax.all_to_all(back, "dp", 0, 0, tiled=True).reshape(entries, shard_cols)
 
+    head_sums = d_sums.reshape(seq_count, 8, MODEL_WIDTH).sum(0)
+    d_bias_out, d_bias_down = jnp.sum(d_one, 0), jnp.sum(d_two, 0)
+    d_bias_ups = [jnp.sum(d_up, 0) for d_up in d_ups]
     d_positions = jnp.sum(d_embedded.reshape(seq_count, MAXLEN, MODEL_WIDTH), 0)
     part = MODEL_WIDTH // inner
     part_positions = columns_sum(lambda half: half_columns(half, d_positions), lambda: d_positions)
@@ -582,23 +596,24 @@
         reduced.append(rows_sum(block, scatter_orders[color])[0])
     own_positions = reduced[0][local_rows:]
     reduced[0] = reduced[0][:local_rows]
-    sums = d_sums.reshape(seq_count, 8, MODEL_WIDTH).sum(0)
-    d_vectors = jnp.concatenate(
-        [
-            d_gain_zero,
-            d_bias_zero,
-            sums[0],
-            sums[1],
-            jnp.sum(d_one, 0),
-            jnp.sum(d_two, 0),
-            d_gain_one,
-            d_bias_one,
-            d_gain_two,
-            d_bias_two,
-            jnp.sum(d_ups[0], 0),
-            jnp.sum(d_ups[1], 0),
-        ]
-    )
+    vector_rows = [
+        d_gain_zero,
+        d_bias_zero,
+        head_sums[0],
+        head_sums[1],
+        d_bias_out,
+        d_bias_down,
+        d_gain_one,
+        d_bias_one,
+        d_gain_two,
+        d_bias_two,
+    ]
+    for sums in d_bias_ups:
+        vector_rows += [sums[k * MODEL_WIDTH : (k + 1) * MODEL_WIDTH] for k in range(PIECE // MODEL_WIDTH)]
+    row_index = jnp.arange(len(vector_rows))[:, None]
+    d_vectors = jnp.zeros((len(vector_rows), MODEL_WIDTH), F32)
+    for k, row in enumerate(vector_rows):
+        d_vectors = jnp.where(row_index == k, row[None, :], d_vectors)
     vector_share = d_vectors.size // devices
 
     def to_columns(values):
@@ -705,7 +720,7 @@
         own_row_sums / widths[None, :] + FLOOR_SQUARE
     )
     scaled_grad = grad_layers * over_columns(lax.rsqrt(own_groups(own_layer_rows)), groups)
-    weight_groups = jnp.sum(by_group(layers[0] * layers[0]), 0)
+    weight_groups = by_group(layer_column_squares)
     lead = 1024
     payload = jnp.concatenate(
         [
@@ -714,8 +729,13 @@
             jnp.sum(scaled_grad * scaled_grad, 0),
         ]
     )
+    payload = jnp.concatenate([payload.reshape(-1, 128), padded(own_positions.reshape(-1), 1024).reshape(-1, 128)], 0)
     payload, _ = lax.optimization_barrier((payload, embed_stats))
-    stats = everyone(payload.reshape(-1, 128), "dp", outer).reshape(outer, -1)
+    stats_rows = (lead + 2 * local_cols) // 128
+    stats = everyone(payload, "dp", outer)
+    stats, pos_stats = stats[:, :stats_rows].reshape(outer, -1), stats[:, stats_rows:].reshape(outer, -1)
+    pos_stats = pos_stats[:, : own_positions.size].reshape(MAXLEN, part)
+    grad_pos = jnp.concatenate(gather_list(pos_stats, "fsdp", inner), 1)
     row_stats = stats[:, : local_rows * 6].reshape(MODEL_WIDTH, 6)
     layer_rows_new = DECAY_RATE * layer_rows[0] + (1.0 - DECAY_RATE) * (
         row_stats.T / widths[:, None] + FLOOR_SQUARE
@@ -748,13 +768,11 @@
     share = -(-shard_rows // inner)
     dense_pad = jnp.pad(own_dense, (0, share * inner - shard_rows))
     own_share = lax.dynamic_slice_in_dim(dense_pad, inner_index * share, share)
-    flat_part = padded(jnp.concatenate([own_vectors, own_share]), 8 * part).reshape(-1, part)
-    pos_rows_count = own_positions.shape[0]
-    payload, _ = lax.optimization_barrier((jnp.concatenate([own_positions, flat_part], 0), stats))
+    flat_part = padded(jnp.concatenate([own_vectors, own_share]), 1024).reshape(-1, 128)
+    payload, _ = lax.optimization_barrier((flat_part, stats))
     spread = everyone(payload, "dp", outer)
     spread = gather_list(spread, "fsdp", inner)
-    grad_pos = jnp.concatenate([values[:, :pos_rows_count].reshape(MAXLEN, part) for values in spread], 1)
-    flats = [values[:, pos_rows_count:].reshape(outer, -1) for values in spread]
+    flats = [values.reshape(outer, -1) for values in spread]
     grad_vectors = jnp.stack([values[:, :vector_share] for values in flats], 1).reshape(norm_vectors.shape)
     embed_row_sum = jnp.concatenate([values[:, vector_share : vector_share + share] for values in flats], 1)
     embed_row_sum = embed_row_sum[:, :shard_rows].reshape(-1)
@@ -762,13 +780,13 @@
 
     grad_head = lax.dot_general(all_pooled, d_projected, CONTRACT_ROWS, precision=EXACT_PRECISION)
     head_update, head_rows_new, head_cols_new = factored_step(grad_head, head_rows, head_cols)
-    head_new, head_spread = apply_update(head_weight, head_update)
+    head_new, head_spread = apply_update(head_weight, head_update, head_square)
     pos_update, pos_rows_new, pos_cols_new = factored_step(grad_pos, pos_rows, pos_cols)
-    positions_new, pos_spread = apply_update(positions, pos_update)
+    positions_new, pos_spread = apply_update(positions, pos_update, pos_square)
     vector_update, vector_moment_new = plain_step(grad_vectors, vector_moment)
-    vectors_new, vector_spread = apply_update(norm_vectors, vector_update)
+    vectors_new, vector_spread = apply_update(norm_vectors, vector_update, vector_square)
     scale_update, scale_moment_new = plain_step(grad_scale, scale_moment)
-    log_scale_new, scale_spread = apply_update(log_scale, scale_update)
+    log_scale_new, scale_spread = apply_update(log_scale, scale_update, log_scale * log_scale)
     update_rms = jnp.concatenate(
         [jnp.stack([embed_spread, head_spread, pos_spread, vector_spread, scale_spread]), spreads]
     )

time: 717 us -> 704 us (0.982)
  waiting for transfers between devices: 198 us -> 179 us
    all_to_all x3, waiting for transfers between devices: 18.1 us -> 4.86 us  [everyone(): lax.all_to_all(jnp.broadcast_to(values[None], (size,) + values.shape), ax...]
    unnamed x233 -> x290, local copies, waits for them, and re-layouts: 28.2 us -> 22.2 us
    ppermute x55 -> x56, waiting for transfers between devices: 180 us -> 174 us  [swap_by(): return lax.ppermute(values, axis, [(i, i ^ mask) for i in range(size)])]
    ppermute x55 -> x56, starting transfers between devices: 51.1 us -> 52.6 us  [swap_by(): return lax.ppermute(values, axis, [(i, i ^ mask) for i in range(size)])]
  transfers between devices with their start and end apart: 62 -> 63, of which waited for: 24 -> 24; matrix products, arithmetic and copies ran while one was open for 24% -> 29% of each run, Pallas kernels for 9% -> 14%
where the time goes in v1:
time: 704 us; the launch traced here: 697 us
  waiting for transfers between devices  179 us (25%)
  matrix products  117 us (17%)
  other arithmetic  112 us (16%)
  Pallas kernels  103 us (15%)
  starting transfers between devices  92.3 us (13%)
  local copies, waits for them, and re-layouts  75.7 us (11%)
  between operations  17.5 us (2%)
    ppermute x56, waiting for transfers between devices, swap_by(): return lax.ppermute(values, axis, [(i, i ^ mask) for i in range(size)])  174 us
    dot_general x31, matrix products, dot(): return lax.dot_general(left, right, dims, preferred_element_type=F32)  110 us
    ppermute x56, starting transfers between devices, swap_by(): return lax.ppermute(values, axis, [(i, i ^ mask) for i in range(size)])  52.6 us
    pallas_call x2, Pallas kernels, attend_back(): pl.pallas_call(functools.partial(attention_back_kernel, seq), grid_spec=p...  34.9 us
    pallas_call x1, Pallas kernels, table_update(): pl.pallas_call(table_kernel, grid_spec=pltpu.PrefetchScalarGridSpec(num_s...  29.9 us
    unnamed x290, local copies, waits for them, and re-layouts  22.2 us
    all_to_all x3, starting transfers between devices, everyone(): lax.all_to_all(jnp.broadcast_to(values[None], (size,) + values.shape), ax...  17.4 us
    pallas_call x1, Pallas kernels, attend(): pl.pallas_call(attention_kernel, grid_spec=pltpu.PrefetchScalarGridSpec(n...  16.1 us
  transfers between devices with their start and end apart: 63, of which 24 were waited for; matrix products, arithmetic and copies ran while one was open for 29% of the time, Pallas kernels for 14%

profile of v1, /device:TPU:0, one launch (start us, length us, event | category | flops | bytes accessed | tf_op | source)
XLA Modules:
  0.0 696.8 jit_solution(10048943747455756565)
XLA Ops:
  3.7 8.3 %all-to-all-start = ((s32[16,1,64]{2,1,0:T(1,128)}), s32[16,1,64]{2,1,0:T(1,128)S(1)}, u32[]{:S(2)}, u32[]{:S(2)}) async-start(s32[16,1,64]{2,1,0:T(1,128)} %all_to_all.26), calls=%async_computation | async-start | bytes 16384 | tf_op jit(solution)/shard_map/all_to_all | solution.py:413
  23.8 11.9 %multiply_reduce_fusion = f32[]{:T(128)} fusion(f32[15632,384]{1,0:T(8,128)} %table_ref.3), kind=kLoop, calls=%fused_computation | loop fusion | flops 12005375 | bytes 24010756 | tf_op jit(solution)/shard_map/reduce_sum | solution.py:651
  41.1 14.4 %take_rows.1 = bf16[2048,384]{1,0:T(8,128)(2,1)} custom-call(s32[2048]{0:T(1024)} %reshape.2260.wanted, f32[15632,384]{1,0:T(8,128)} %table_ref.3), custom_call_target="tpu_custom_call" | custom-call | tf_op jit(solution)/shard_map/take_rows/pallas_call | solution.py:224
  55.6 5.8 convert_reduce_fusion
  61.5 5.2 all-to-all-start.1
  83.5 10.9 %collective-permute-done.8 = bf16[2,1,1,1,48,1536]{5,4,0,3,2,1:T(8,128)(2,1)S(1)} collective-permute-done((bf16[2,1,1,1,48,1536]{5,4,0,3,2,1:T(8,128)(2,1)S(1)}, bf16[2,1,1,1,48,1536]{5,4,0,3,2,1:T(8,128)(2,1)S(1)}, u32[]{:S(2)}, u32[]{:S(2)}) %collective-permute-start.8) | collective-permute-done | bytes 294944 | tf_op jit(solution)/shard_map/ppermute | solution.py:60
  97.0 16.4 %collective-permute-done.9 = bf16[2,1,1,2,48,1536]{5,4,0,3,2,1:T(8,128)(2,1)S(1)} collective-permute-done((bf16[2,1,1,2,48,1536]{5,4,0,3,2,1:T(8,128)(2,1)S(1)}, bf16[2,1,1,2,48,1536]{5,4,0,3,2,1:T(8,128)(2,1)S(1)}, u32[]{:S(2)}, u32[]{:S(2)}) %collective-permute-start.9) | collective-permute-done | bytes 589856 | tf_op jit(solution)/shard_map/ppermute | solution.py:60
  117.7 36.7 %collective-permute-done.4 = bf16[2,2,1,1,48,1536]{5,4,3,2,1,0:T(8,128)(2,1)S(1)} collective-permute-done((bf16[2,2,1,1,48,1536]{5,4,3,2,1,0:T(8,128)(2,1)S(1)}, bf16[2,2,1,1,48,1536]{5,4,3,2,1,0:T(8,128)(2,1)S(1)}, u32[]{:S(2)}, u32[]{:S(2)}) %collective-permute-start.4) | collective-permute-done | bytes 589856 | tf_op jit(solution)/shard_map/ppermute | solution.py:60
  161.6 20.8 %collective-permute-done.5 = bf16[2,2,2,1,48,1536]{5,4,3,2,1,0:T(8,128)(2,1)} collective-permute-done((bf16[2,2,2,1,48,1536]{5,4,3,2,1,0:T(8,128)(2,1)}, bf16[2,2,2,1,48,1536]{5,4,3,2,1,0:T(8,128)(2,1)}, u32[]{:S(2)}, u32[]{:S(2)}) %collective-permute-start.5) | collective-permute-done | bytes 1179680 | tf_op jit(solution)/shard_map/ppermute | solution.py:60
  188.0 4.3 maximum_select_fusion.2
  206.1 4.0 add_convert_fusion.q_ref.k_ref
  210.2 16.1 %attend.1 = bf16[1024,768]{1,0:T(8,128)(2,1)} custom-call(s32[2]{0:T(128)} %lengths.2, bf16[1024,1536]{1,0:T(8,128)(2,1)} %add_convert_fusion.q_ref.k_ref, bf16[1024,1536]{1,0:T(8,128)(2,1)} %add_convert_fusion.q_ref.k_ref, bf16[1024,768]{1,0:T(8,128)(2,1)} %add_convert_fusion.1.v_ref), custom_call_target="tpu_custom_call" | custom-call | tf_op jit(solution)/shard_map/attend/pallas_call | solution.py:150
  233.1 5.4 multiply_convert_fusion
  238.5 7.0 multiply_convert_fusion.1
  245.5 5.4 fusion.82
  251.0 4.9 fusion.187
  258.3 6.0 all-to-all-start.2
  268.4 4.9 all-to-all-done.2
  274.0 8.0 %contrast.1 = (f32[64,768]{1,0:T(8,128)}, f32[64,768]{1,0:T(8,128)}, f32[8,128]{1,0:T(8,128)}) custom-call(f32[1]{0:T(128)} %bitcast.385.scale_ref, f32[64,768]{1,0:T(8,128)} %reshape.2266.pooled_ref, f32[768,768]{1,0:T(8,128)} %head_ref.1), custom_call_target="tpu_custom_call" | custom-call | tf_op jit(solution)/shard_map/contrast/pallas_call | solution.py:340
  288.2 4.1 convolution_convert_fusion
  292.2 6.9 fusion.188
  299.2 6.9 fusion.189
  306.1 4.4 convolution_convert_fusion.1
  310.5 4.5 fusion.76
  315.0 3.7 multiply_reduce_fusion.3
  327.1 17.4 %shard_map.338 = (bf16[1024,768]{1,0:T(8,128)(2,1)}, bf16[1024,768]{1,0:T(8,128)(2,1)}, bf16[1024,768]{1,0:T(8,128)(2,1)}, f32[16,768]{1,0:T(8,128)}) custom-call(s32[2]{0:T(128)} %lengths.2, bf16[1024,1536]{1,0:T(8,128)(2,1)} %add_convert_fusion.q_ref.k_ref, bf16[1024,1536]{1,0:T(8,128)(2,1)} %add_convert_fusion.q_ref.k_ref, ...), custom_call_target="tpu_custom_call" | custom-call | tf_op jit(solution)/shard_map/pallas_call | solution.py:196
  344.5 17.5 %shard_map.339 = (bf16[1024,768]{1,0:T(8,128)(2,1)}, bf16[1024,768]{1,0:T(8,128)(2,1)}, bf16[1024,768]{1,0:T(8,128)(2,1)}, f32[16,768]{1,0:T(8,128)}) custom-call(s32[2]{0:T(128)} %lengths.2, bf16[1024,1536]{1,0:T(8,128)(2,1)} %add_convert_fusion.q_ref.k_ref, ...), custom_call_target="tpu_custom_call", output_to_operand_aliasing={{0}: (5, {}), {1}: (6, {}), {2}: (7, {}), {3}: (8, {})} | custom-call | tf_op jit(solution)/shard_map/pallas_call | solution.py:196
  407.0 3.9 collective-permute-done.39
  414.0 4.8 all-to-all-start.3
  430.8 7.5 %collective-permute-done.26 = bf16[8,48,384]{2,1,0:T(8,128)(2,1)S(1)} collective-permute-done((bf16[8,48,384]{2,1,0:T(8,128)(2,1)S(1)}, bf16[8,48,384]{2,1,0:T(8,128)(2,1)S(1)}, u32[]{:S(2)}, u32[]{:S(2)}) %collective-permute-start.26) | collective-permute-done | bytes 294944 | tf_op jit(solution)/shard_map/ppermute | solution.py:60
  439.5 11.9 %collective-permute-done.31 = bf16[8,48,384]{2,1,0:T(8,128)(2,1)S(1)} collective-permute-done((bf16[8,48,384]{2,1,0:T(8,128)(2,1)S(1)}, bf16[8,48,384]{2,1,0:T(8,128)(2,1)S(1)}, u32[]{:S(2)}, u32[]{:S(2)}) %collective-permute-start.31) | collective-permute-done | bytes 294944 | tf_op jit(solution)/shard_map/ppermute | solution.py:60
  467.2 5.1 collective-permute-done.23
  478.3 5.4 convert_add_fusion.1
  486.3 4.3 convert_add_fusion
  494.4 17.9 %collective-permute-done.42 = bf16[384,1536]{1,0:T(8,128)(2,1)S(1)} collective-permute-done((bf16[384,1536]{1,0:T(8,128)(2,1)S(1)}, bf16[384,1536]{1,0:T(8,128)(2,1)S(1)}, u32[]{:S(2)}, u32[]{:S(2)}) %collective-permute-start.42) | collective-permute-done | bytes 1179680 | tf_op jit(solution)/shard_map/ppermute | solution.py:60
  514.6 4.7 collective-permute-done.47
  520.8 6.2 multiply_reduce_fusion.5
  535.1 4.0 all-to-all-start.4
  539.1 5.4 collective-permute-done.43
  549.8 5.8 collective-permute-done.44
  558.9 9.3 %collective-permute-done.45 = bf16[48,1536]{1,0:T(8,128)(2,1)S(1)} collective-permute-done((bf16[48,1536]{1,0:T(8,128)(2,1)S(1)}, bf16[48,1536]{1,0:T(8,128)(2,1)S(1)}, u32[]{:S(2)}, u32[]{:S(2)}) %collective-permute-start.45) | collective-permute-done | bytes 147488 | tf_op jit(solution)/shard_map/ppermute | solution.py:60
  577.8 3.9 concatenate.680
  582.9 4.7 all-to-all-start.5
  587.7 4.6 multiply_reduce_fusion.17
  598.2 3.7 multiply_subtract_fusion
  608.0 29.9 %table_update.1 = (f32[15632,384]{1,0:T(8,128)}, bf16[15632,384]{1,0:T(8,128)(2,1)}) custom-call(s32[2048]{0:T(1024)} %copy-done.55, s32[9]{0:T(128)} %convert_reduce_fusion.1.starts, f32[15632,384]{1,0:T(8,128)} %table_ref.3, f32[2048,384]{1,0:T(8,128)} %get-tuple-element.259.update_ref, f32[1,384]{1,0:T(1,128)} %broadcast_in_dim.438.scale_ref), custom_call_target="tpu_custom_call" | custom-call | tf_op jit(solution)/shard_map/table_update/pallas_call | solution.py:256
  641.6 6.7 all-to-all-start.6
  654.8 5.2 concatenate.685
  (671 shorter events, 262.5 us)
Async XLA Ops:
  3.7 32.6 %all-to-all-start = ((s32[16,1,64]{2,1,0:T(1,128)}), s32[16,1,64]{2,1,0:T(1,128)S(1)}, u32[]{:S(2)}, u32[]{:S(2)}) async-start(s32[16,1,64]{2,1,0:T(1,128)} %all_to_all.26), calls=%async_computation | async-start | bytes 16384 | tf_op jit(solution)/shard_map/all_to_all | solution.py:413
  14.0 62.3 %collective-permute-start.7 = (bf16[1,1,1,1,48,1536]{5,4,0,3,2,1:T(8,128)(2,1)}, bf16[1,1,1,1,48,1536]{5,4,0,3,2,1:T(8,128)(2,1)S(1)}, u32[]{:S(2)}, u32[]{:S(2)}) collective-permute-start(bf16[1,1,1,1,48,1536]{5,4,0,3,2,1:T(8,128)(2,1)} %get-tuple-element.284), channel_id=1, source_target_pairs={{0,16},{2,18},{4,20},{6,22},{8,24},{10,26},{12,28},{14,30},{16,0},... | collective-permute-start | bytes 442376 | tf_op jit(solution)/shard_map/ppermute | solution.py:60
  16.8 62.5 %collective-permute-start.2 = (bf16[1,1,1,1,48,1536]{5,4,3,2,1,0:T(8,128)(2,1)}, bf16[1,1,1,1,48,1536]{5,4,3,2,1,0:T(8,128)(2,1)S(1)}, u32[]{:S(2)}, u32[]{:S(2)}) collective-permute-start(bf16[1,1,1,1,48,1536]{5,4,3,2,1,0:T(8,128)(2,1)} %get-tuple-element.283), channel_id=1, source_target_pairs={{0,16},{2,18},{4,20},{6,22},{8,24},{10,26},{12,28},{14,30},{16,0},... | collective-permute-start | bytes 442376 | tf_op jit(solution)/shard_map/ppermute | solution.py:60
  16.9 65.0 %collective-permute-start.12 = (bf16[1,1,1,1,48,1536]{5,4,3,2,1,0:T(8,128)(2,1)S(1)}, bf16[1,1,1,1,48,1536]{5,4,3,2,1,0:T(8,128)(2,1)S(1)}, u32[]{:S(2)}, u32[]{:S(2)}) collective-permute-start(bf16[1,1,1,1,48,1536]{5,4,3,2,1,0:T(8,128)(2,1)S(1)} %get-tuple-element.282), channel_id=1, source_target_pairs={{0,16},{2,18},{4,20},{6,22},{8,24},{10,26},{12,28},{14,30},{16,0},... | collective-permute-start | bytes 442376 | tf_op jit(solution)/shard_map/ppermute | solution.py:60
  61.5 99.7 %all-to-all-start.1 = ((bf16[16,2,64,384]{3,2,1,0:T(8,128)(2,1)}), bf16[16,2,64,384]{3,2,1,0:T(8,128)(2,1)S(1)}, u32[]{:S(2)}, u32[]{:S(2)}) async-start(bf16[16,2,64,384]{3,2,1,0:T(8,128)(2,1)} %bitcast.397), calls=%async_computation.1 | async-start | bytes 3145728 | tf_op jit(solution)/shard_map/all_to_all | solution.py:441
  77.4 17.0 %collective-permute-start.8 = (bf16[2,1,1,1,48,1536]{5,4,0,3,2,1:T(8,128)(2,1)S(1)}, bf16[2,1,1,1,48,1536]{5,4,0,3,2,1:T(8,128)(2,1)S(1)}, u32[]{:S(2)}, u32[]{:S(2)}) collective-permute-start(bf16[2,1,1,1,48,1536]{5,4,0,3,2,1:T(8,128)(2,1)S(1)} %maximum_select_fusion.13), channel_id=1, source_target_pairs={{0,2},{2,0},{4,6},{6,4},{8,10},{10,8},{12,14},{14,12},{16,18},{18,... | collective-permute-start | bytes 884744 | tf_op jit(solution)/shard_map/ppermute | solution.py:60
  80.4 35.8 %collective-permute-start.3 = (bf16[2,1,1,1,48,1536]{5,4,3,2,1,0:T(8,128)(2,1)S(1)}, bf16[2,1,1,1,48,1536]{5,4,3,2,1,0:T(8,128)(2,1)S(1)}, u32[]{:S(2)}, u32[]{:S(2)}) collective-permute-start(bf16[2,1,1,1,48,1536]{5,4,3,2,1,0:T(8,128)(2,1)S(1)} %bitcast_select_fusion.1), channel_id=1, source_target_pairs={{0,8},{2,10},{4,12},{6,14},{8,0},{10,2},{12,4},{14,6},{16,24},{18,... | collective-permute-start | bytes 884744 | tf_op jit(solution)/shard_map/ppermute | solution.py:60
  82.0 34.4 %collective-permute-start.13 = (bf16[2,1,1,1,48,1536]{5,4,3,2,1,0:T(8,128)(2,1)S(1)}, bf16[2,1,1,1,48,1536]{5,4,3,2,1,0:T(8,128)(2,1)S(1)}, u32[]{:S(2)}, u32[]{:S(2)}) collective-permute-start(bf16[2,1,1,1,48,1536]{5,4,3,2,1,0:T(8,128)(2,1)S(1)} %bitcast_select_fusion), channel_id=1, source_target_pairs={{0,4},{2,6},{4,0},{6,2},{8,12},{10,14},{12,8},{14,10},{16,20},{18,... | collective-permute-start | bytes 884744 | tf_op jit(solution)/shard_map/ppermute | solution.py:60
  94.5 18.9 %collective-permute-start.9 = (bf16[2,1,1,2,48,1536]{5,4,0,3,2,1:T(8,128)(2,1)S(1)}, bf16[2,1,1,2,48,1536]{5,4,0,3,2,1:T(8,128)(2,1)S(1)}, u32[]{:S(2)}, u32[]{:S(2)}) collective-permute-start(bf16[2,1,1,2,48,1536]{5,4,0,3,2,1:T(8,128)(2,1)S(1)} %maximum_select_fusion.9), channel_id=1, source_target_pairs={{0,8},{2,10},{4,12},{6,14},{8,0},{10,2},{12,4},{14,6},{16,24},{18,... | collective-permute-start | bytes 1769480 | tf_op jit(solution)/shard_map/ppermute | solution.py:60
  113.6 42.6 %collective-permute-start.10 = (bf16[2,2,1,2,48,1536]{5,4,0,3,2,1:T(8,128)(2,1)S(1)}, bf16[2,2,1,2,48,1536]{5,4,0,3,2,1:T(8,128)(2,1)S(1)}, u32[]{:S(2)}, u32[]{:S(2)}) collective-permute-start(bf16[2,2,1,2,48,1536]{5,4,0,3,2,1:T(8,128)(2,1)S(1)} %maximum_select_fusion.4), channel_id=1, source_target_pairs={{0,4},{2,6},{4,0},{6,2},{8,12},{10,14},{12,8},{14,10},{16,20},{18,... | collective-permute-start | bytes 3538952 | tf_op jit(solution)/shard_map/ppermute | solution.py:60
  116.2 38.1 %collective-permute-start.4 = (bf16[2,2,1,1,48,1536]{5,4,3,2,1,0:T(8,128)(2,1)S(1)}, bf16[2,2,1,1,48,1536]{5,4,3,2,1,0:T(8,128)(2,1)S(1)}, u32[]{:S(2)}, u32[]{:S(2)}) collective-permute-start(bf16[2,2,1,1,48,1536]{5,4,3,2,1,0:T(8,128)(2,1)S(1)} %maximum_select_fusion.7), channel_id=1, source_target_pairs={{0,4},{2,6},{4,0},{6,2},{8,12},{10,14},{12,8},{14,10},{16,20},{18,... | collective-permute-start | bytes 1769480 | tf_op jit(solution)/shard_map/ppermute | solution.py:60
  116.5 41.7 %collective-permute-start.14 = (bf16[2,1,2,1,48,1536]{5,4,3,2,1,0:T(8,128)(2,1)S(1)}, bf16[2,1,2,1,48,1536]{5,4,3,2,1,0:T(8,128)(2,1)S(1)}, u32[]{:S(2)}, u32[]{:S(2)}) collective-permute-start(bf16[2,1,2,1,48,1536]{5,4,3,2,1,0:T(8,128)(2,1)S(1)} %maximum_select_fusion.11), channel_id=1, source_target_pairs={{0,2},{2,0},{4,6},{6,4},{8,10},{10,8},{12,14},{14,12},{16,18},{18,... | collective-permute-start | bytes 1769480 | tf_op jit(solution)/shard_map/ppermute | solution.py:60
  155.5 27.0 %collective-permute-start.5 = (bf16[2,2,2,1,48,1536]{5,4,3,2,1,0:T(8,128)(2,1)}, bf16[2,2,2,1,48,1536]{5,4,3,2,1,0:T(8,128)(2,1)}, u32[]{:S(2)}, u32[]{:S(2)}) collective-permute-start(bf16[2,2,2,1,48,1536]{5,4,3,2,1,0:T(8,128)(2,1)} %maximum_select_fusion.3), channel_id=1, source_target_pairs={{0,2},{2,0},{4,6},{6,4},{8,10},{10,8},{12,14},{14,12},{16,18},{18,... | collective-permute-start | bytes 3538952 | tf_op jit(solution)/shard_map/ppermute | solution.py:60
  158.2 40.1 %collective-permute-start.11 = (bf16[768,1536]{1,0:T(8,128)(2,1)}, bf16[768,1536]{1,0:T(8,128)(2,1)}, u32[]{:S(2)}, u32[]{:S(2)}) collective-permute-start(bf16[768,1536]{1,0:T(8,128)(2,1)} %bitcast.26), channel_id=1, source_target_pairs={{0,1},{1,0},{2,3},{3,2},{4,5},{5,4},{6,7},{7,6},{8,9},{9,8},{10,11... | collective-permute-start | bytes 7077896 | tf_op jit(solution)/shard_map/ppermute | solution.py:60
  159.3 28.7 %collective-permute-start.15 = (bf16[2,1,2,2,48,1536]{5,4,3,2,1,0:T(8,128)(2,1)}, bf16[2,1,2,2,48,1536]{5,4,3,2,1,0:T(8,128)(2,1)}, u32[]{:S(2)}, u32[]{:S(2)}) collective-permute-start(bf16[2,1,2,2,48,1536]{5,4,3,2,1,0:T(8,128)(2,1)} %maximum_select_fusion.5), channel_id=1, source_target_pairs={{0,8},{2,10},{4,12},{6,14},{8,0},{10,2},{12,4},{14,6},{16,24},{18,... | collective-permute-start | bytes 3538952 | tf_op jit(solution)/shard_map/ppermute | solution.py:60
  161.3 31.0 %collective-permute-start.1 = (bf16[1024,384]{1,0:T(8,128)(2,1)S(1)}, bf16[1024,384]{1,0:T(8,128)(2,1)S(1)}, u32[]{:S(2)}, u32[]{:S(2)}) collective-permute-start(bf16[1024,384]{1,0:T(8,128)(2,1)S(1)} %bitcast.445), channel_id=1, source_target_pairs={{0,1},{1,0},{2,3},{3,2},{4,5},{5,4},{6,7},{7,6},{8,9},{9,8},{10,11... | collective-permute-start | bytes 2359304 | tf_op jit(solution)/shard_map/ppermute | solution.py:60
  185.4 17.9 %collective-permute-start.6 = (bf16[768,1536]{1,0:T(8,128)(2,1)S(1)}, bf16[768,1536]{1,0:T(8,128)(2,1)S(1)}, u32[]{:S(2)}, u32[]{:S(2)}) collective-permute-start(bf16[768,1536]{1,0:T(8,128)(2,1)S(1)} %bitcast.387), channel_id=1, source_target_pairs={{0,1},{1,0},{2,3},{3,2},{4,5},{5,4},{6,7},{7,6},{8,9},{9,8},{10,11... | collective-permute-start | bytes 7077896 | tf_op jit(solution)/shard_map/ppermute | solution.py:60
  192.3 46.2 %collective-permute-start.16 = (bf16[768,1536]{1,0:T(8,128)(2,1)}, bf16[768,1536]{1,0:T(8,128)(2,1)}, u32[]{:S(2)}, u32[]{:S(2)}) collective-permute-start(bf16[768,1536]{1,0:T(8,128)(2,1)} %bitcast.37), channel_id=1, source_target_pairs={{0,1},{1,0},{2,3},{3,2},{4,5},{5,4},{6,7},{7,6},{8,9},{9,8},{10,11... | collective-permute-start | bytes 7077896 | tf_op jit(solution)/shard_map/ppermute | solution.py:60
  258.3 15.0 %all-to-all-start.2 = ((f32[32,2,768]{2,1,0:T(2,128)}), f32[32,2,768]{2,1,0:T(2,128)S(1)}, u32[]{:S(2)}, u32[]{:S(2)}) async-start(f32[32,2,768]{2,1,0:T(2,128)} %broadcast_in_dim.382), calls=%async_computation.2 | async-start | bytes 393216 | tf_op jit(solution)/shard_map/all_to_all | solution.py:118
  326.0 54.1 %collective-permute-start.36 = (bf16[768,384]{1,0:T(8,128)(2,1)}, bf16[768,384]{1,0:T(8,128)(2,1)}, u32[]{:S(2)}, u32[]{:S(2)}) collective-permute-start(bf16[768,384]{1,0:T(8,128)(2,1)} %convolution_convert_fusion.3), channel_id=1, source_target_pairs={{0,1},{1,0},{2,3},{3,2},{4,5},{5,4},{6,7},{7,6},{8,9},{9,8},{10,11... | collective-permute-start | bytes 1769480 | tf_op jit(solution)/shard_map/ppermute | solution.py:60
  326.6 151.7 %collective-permute-start.41 = (bf16[768,1536]{1,0:T(8,128)(2,1)}, bf16[768,1536]{1,0:T(8,128)(2,1)}, u32[]{:S(2)}, u32[]{:S(2)}) collective-permute-start(bf16[768,1536]{1,0:T(8,128)(2,1)} %convolution_convert_fusion.1), channel_id=1, source_target_pairs={{0,1},{1,0},{2,3},{3,2},{4,5},{5,4},{6,7},{7,6},{8,9},{9,8},{10,11... | collective-permute-start | bytes 7077896 | tf_op jit(solution)/shard_map/ppermute | solution.py:60
  326.6 158.2 %collective-permute-start.46 = (bf16[768,1536]{1,0:T(8,128)(2,1)}, bf16[768,1536]{1,0:T(8,128)(2,1)}, u32[]{:S(2)}, u32[]{:S(2)}) collective-permute-start(bf16[768,1536]{1,0:T(8,128)(2,1)} %convolution_convert_fusion), channel_id=1, source_target_pairs={{0,1},{1,0},{2,3},{3,2},{4,5},{5,4},{6,7},{7,6},{8,9},{9,8},{10,11... | collective-permute-start | bytes 7077896 | tf_op jit(solution)/shard_map/ppermute | solution.py:60
  375.6 9.3 %collective-permute-start.17 = (bf16[1024,384]{1,0:T(8,128)(2,1)}, bf16[1024,384]{1,0:T(8,128)(2,1)}, u32[]{:S(2)}, u32[]{:S(2)}) collective-permute-start(bf16[1024,384]{1,0:T(8,128)(2,1)} %get-tuple-element.269), channel_id=1, source_target_pairs={{0,1},{1,0},{2,3},{3,2},{4,5},{5,4},{6,7},{7,6},{8,9},{9,8},{10,11... | collective-permute-start | bytes 2359304 | tf_op jit(solution)/shard_map/ppermute | solution.py:60
  383.0 16.4 %collective-permute-start.37 = (bf16[384,384]{1,0:T(8,128)(2,1)S(1)}, bf16[384,384]{1,0:T(8,128)(2,1)}, u32[]{:S(2)}, u32[]{:S(2)}) collective-permute-start(bf16[384,384]{1,0:T(8,128)(2,1)S(1)} %bitcast.461), channel_id=1, source_target_pairs={{0,8},{2,10},{4,12},{6,14},{8,0},{10,2},{12,4},{14,6},{16,24},{18,... | collective-permute-start | bytes 884744 | tf_op jit(solution)/shard_map/ppermute | solution.py:60
  389.2 31.9 %collective-permute-start.25 = (bf16[768,384]{1,0:T(8,128)(2,1)}, bf16[768,384]{1,0:T(8,128)(2,1)}, u32[]{:S(2)}, u32[]{:S(2)}) collective-permute-start(bf16[768,384]{1,0:T(8,128)(2,1)} %convolution_convert_fusion.5), channel_id=1, source_target_pairs={{0,1},{1,0},{2,3},{3,2},{4,5},{5,4},{6,7},{7,6},{8,9},{9,8},{10,11... | collective-permute-start | bytes 1769480 | tf_op jit(solution)/shard_map/ppermute | solution.py:60
  394.5 25.1 %collective-permute-start.20 = (bf16[512,384]{1,0:T(8,128)(2,1)}, bf16[512,384]{1,0:T(8,128)(2,1)}, u32[]{:S(2)}, u32[]{:S(2)}) collective-permute-start(bf16[512,384]{1,0:T(8,128)(2,1)} %dynamic-slice_convert_fusion.4), channel_id=1, source_target_pairs={{0,1},{1,0},{2,3},{3,2},{4,5},{5,4},{6,7},{7,6},{8,9},{9,8},{10,11... | collective-permute-start | bytes 1179656 | tf_op jit(solution)/shard_map/ppermute | solution.py:60
  410.9 7.9 %collective-permute-start.40 = (bf16[48,384]{1,0:T(8,128)(2,1)S(1)}, bf16[48,384]{1,0:T(8,128)(2,1)S(1)}, u32[]{:S(2)}, u32[]{:S(2)}) collective-permute-start(bf16[48,384]{1,0:T(8,128)(2,1)S(1)} %fusion.130), channel_id=1, source_target_pairs={{0,16},{2,18},{4,20},{6,22},{8,24},{10,26},{12,28},{14,30},{16,0},... | collective-permute-start | bytes 110600 | tf_op jit(solution)/shard_map/ppermute | solution.py:60
  414.0 105.8 %all-to-all-start.3 = ((bf16[16,2,64,384]{3,2,1,0:T(8,128)(2,1)}), bf16[16,2,64,384]{3,2,1,0:T(8,128)(2,1)}, u32[]{:S(2)}, u32[]{:S(2)}) async-start(bf16[16,2,64,384]{3,2,1,0:T(8,128)(2,1)} %pad_maximum_fusion), calls=%async_computation.3 | async-start | bytes 3145728 | tf_op jit(solution)/shard_map/all_to_all | solution.py:580
  419.5 8.6 %collective-permute-start.19 = (bf16[768,384]{1,0:T(8,128)(2,1)}, bf16[768,384]{1,0:T(8,128)(2,1)S(1)}, u32[]{:S(2)}, u32[]{:S(2)}) collective-permute-start(bf16[768,384]{1,0:T(8,128)(2,1)} %convolution_convert_fusion.6), channel_id=1, source_target_pairs={{0,1},{1,0},{2,3},{3,2},{4,5},{5,4},{6,7},{7,6},{8,9},{9,8},{10,11... | collective-permute-start | bytes 1769480 | tf_op jit(solution)/shard_map/ppermute | solution.py:60
  423.6 14.7 %collective-permute-start.26 = (bf16[8,48,384]{2,1,0:T(8,128)(2,1)S(1)}, bf16[8,48,384]{2,1,0:T(8,128)(2,1)S(1)}, u32[]{:S(2)}, u32[]{:S(2)}) collective-permute-start(bf16[8,48,384]{2,1,0:T(8,128)(2,1)S(1)} %bitcast.459), channel_id=1, source_target_pairs={{0,4},{2,6},{4,0},{6,2},{8,12},{10,14},{12,8},{14,10},{16,20},{18,... | collective-permute-start | bytes 884744 | tf_op jit(solution)/shard_map/ppermute | solution.py:60
  426.6 24.9 %collective-permute-start.31 = (bf16[8,48,384]{2,1,0:T(8,128)(2,1)S(1)}, bf16[8,48,384]{2,1,0:T(8,128)(2,1)S(1)}, u32[]{:S(2)}, u32[]{:S(2)}) collective-permute-start(bf16[8,48,384]{2,1,0:T(8,128)(2,1)S(1)} %bitcast.460), channel_id=1, source_target_pairs={{0,8},{2,10},{4,12},{6,14},{8,0},{10,2},{12,4},{14,6},{16,24},{18,... | collective-permute-start | bytes 884744 | tf_op jit(solution)/shard_map/ppermute | solution.py:60
  429.2 31.0 %collective-permute-start.21 = (bf16[8,80,384]{2,1,0:T(8,128)(2,1)S(1)}, bf16[8,80,384]{2,1,0:T(8,128)(2,1)S(1)}, u32[]{:S(2)}, u32[]{:S(2)}) collective-permute-start(bf16[8,80,384]{2,1,0:T(8,128)(2,1)S(1)} %fusion.110), channel_id=1, source_target_pairs={{0,2},{2,0},{4,6},{6,4},{8,10},{10,8},{12,14},{14,12},{16,18},{18,... | collective-permute-start | bytes 1474568 | tf_op jit(solution)/shard_map/ppermute | solution.py:60
  438.4 15.2 %collective-permute-start.27 = (bf16[4,48,384]{2,1,0:T(8,128)(2,1)S(1)}, bf16[4,48,384]{2,1,0:T(8,128)(2,1)S(1)}, u32[]{:S(2)}, u32[]{:S(2)}) collective-permute-start(bf16[4,48,384]{2,1,0:T(8,128)(2,1)S(1)} %bitcast.464), channel_id=1, source_target_pairs={{0,8},{2,10},{4,12},{6,14},{8,0},{10,2},{12,4},{14,6},{16,24},{18,... | collective-permute-start | bytes 442376 | tf_op jit(solution)/shard_map/ppermute | solution.py:60
  453.6 6.8 collective-permute-start.28
  463.4 11.1 %collective-permute-start.34 = (bf16[1,48,384]{2,1,0:T(8,128)(2,1)S(1)}, bf16[1,48,384]{2,1,0:T(8,128)(2,1)S(1)}, u32[]{:S(2)}, u32[]{:S(2)}) collective-permute-start(bf16[1,48,384]{2,1,0:T(8,128)(2,1)S(1)} %dynamic-slice_convert_fusion.20), channel_id=1, source_target_pairs={{0,16},{2,18},{4,20},{6,22},{8,24},{10,26},{12,28},{14,30},{16,0},... | collective-permute-start | bytes 110600 | tf_op jit(solution)/shard_map/ppermute | solution.py:60
  477.6 14.8 %collective-permute-start.35 = (f32[48,1152]{1,0:T(8,128)S(1)}, f32[48,1152]{1,0:T(8,128)S(1)}, u32[]{:S(2)}, u32[]{:S(2)}) collective-permute-start(f32[48,1152]{1,0:T(8,128)S(1)} %pad_maximum_fusion.4), channel_id=1, source_target_pairs={{0,1},{1,0},{2,3},{3,2},{4,5},{5,4},{6,7},{7,6},{8,9},{9,8},{10,11... | collective-permute-start | bytes 663560 | tf_op jit(solution)/shard_map/ppermute | solution.py:60
  483.9 28.4 %collective-permute-start.42 = (bf16[384,1536]{1,0:T(8,128)(2,1)S(1)}, bf16[384,1536]{1,0:T(8,128)(2,1)S(1)}, u32[]{:S(2)}, u32[]{:S(2)}) collective-permute-start(bf16[384,1536]{1,0:T(8,128)(2,1)S(1)} %bitcast.434), channel_id=1, source_target_pairs={{0,4},{2,6},{4,0},{6,2},{8,12},{10,14},{12,8},{14,10},{16,20},{18,... | collective-permute-start | bytes 3538952 | tf_op jit(solution)/shard_map/ppermute | solution.py:60
  490.9 28.4 %collective-permute-start.47 = (bf16[384,1536]{1,0:T(8,128)(2,1)S(1)}, bf16[384,1536]{1,0:T(8,128)(2,1)S(1)}, u32[]{:S(2)}, u32[]{:S(2)}) collective-permute-start(bf16[384,1536]{1,0:T(8,128)(2,1)S(1)} %bitcast.435), channel_id=1, source_target_pairs={{0,2},{2,0},{4,6},{6,4},{8,10},{10,8},{12,14},{14,12},{16,18},{18,... | collective-permute-start | bytes 3538952 | tf_op jit(solution)/shard_map/ppermute | solution.py:60
  528.0 16.6 %collective-permute-start.43 = (bf16[192,1536]{1,0:T(8,128)(2,1)}, bf16[192,1536]{1,0:T(8,128)(2,1)}, u32[]{:S(2)}, u32[]{:S(2)}) collective-permute-start(bf16[192,1536]{1,0:T(8,128)(2,1)} %bitcast.100), channel_id=1, source_target_pairs={{0,2},{2,0},{4,6},{6,4},{8,10},{10,8},{12,14},{14,12},{16,18},{18,... | collective-permute-start | bytes 1769480 | tf_op jit(solution)/shard_map/ppermute | solution.py:60
  529.4 18.5 %collective-permute-start.48 = (bf16[192,1536]{1,0:T(8,128)(2,1)}, bf16[192,1536]{1,0:T(8,128)(2,1)}, u32[]{:S(2)}, u32[]{:S(2)}) collective-permute-start(bf16[192,1536]{1,0:T(8,128)(2,1)} %bitcast.112), channel_id=1, source_target_pairs={{0,8},{2,10},{4,12},{6,14},{8,0},{10,2},{12,4},{14,6},{16,24},{18,... | collective-permute-start | bytes 1769480 | tf_op jit(solution)/shard_map/ppermute | solution.py:60
  535.1 37.3 %all-to-all-start.4 = ((f32[32,16,128]{2,1,0:T(8,128)}), f32[32,16,128]{2,1,0:T(8,128)}, u32[]{:S(2)}, u32[]{:S(2)}) async-start(f32[32,16,128]{2,1,0:T(8,128)} %bitcast.181), calls=%async_computation.4 | async-start | bytes 524288 | tf_op jit(solution)/shard_map/all_to_all | solution.py:671
  545.9 9.7 %collective-permute-start.44 = (bf16[96,1536]{1,0:T(8,128)(2,1)S(1)}, bf16[96,1536]{1,0:T(8,128)(2,1)S(1)}, u32[]{:S(2)}, u32[]{:S(2)}) collective-permute-start(bf16[96,1536]{1,0:T(8,128)(2,1)S(1)} %bitcast.462), channel_id=1, source_target_pairs={{0,8},{2,10},{4,12},{6,14},{8,0},{10,2},{12,4},{14,6},{16,24},{18,... | collective-permute-start | bytes 884744 | tf_op jit(solution)/shard_map/ppermute | solution.py:60
  549.2 8.2 %collective-permute-start.49 = (bf16[96,1536]{1,0:T(8,128)(2,1)S(1)}, bf16[96,1536]{1,0:T(8,128)(2,1)S(1)}, u32[]{:S(2)}, u32[]{:S(2)}) collective-permute-start(bf16[96,1536]{1,0:T(8,128)(2,1)S(1)} %bitcast.463), channel_id=1, source_target_pairs={{0,4},{2,6},{4,0},{6,2},{8,12},{10,14},{12,8},{14,10},{16,20},{18,... | collective-permute-start | bytes 884744 | tf_op jit(solution)/shard_map/ppermute | solution.py:60
  555.7 12.5 %collective-permute-start.45 = (bf16[48,1536]{1,0:T(8,128)(2,1)S(1)}, bf16[48,1536]{1,0:T(8,128)(2,1)S(1)}, u32[]{:S(2)}, u32[]{:S(2)}) collective-permute-start(bf16[48,1536]{1,0:T(8,128)(2,1)S(1)} %fusion.115), channel_id=1, source_target_pairs={{0,16},{2,18},{4,20},{6,22},{8,24},{10,26},{12,28},{14,30},{16,0},... | collective-permute-start | bytes 442376 | tf_op jit(solution)/shard_map/ppermute | solution.py:60
  557.5 13.7 %collective-permute-start.50 = (bf16[48,1536]{1,0:T(8,128)(2,1)S(1)}, bf16[48,1536]{1,0:T(8,128)(2,1)S(1)}, u32[]{:S(2)}, u32[]{:S(2)}) collective-permute-start(bf16[48,1536]{1,0:T(8,128)(2,1)S(1)} %fusion.116), channel_id=1, source_target_pairs={{0,16},{2,18},{4,20},{6,22},{8,24},{10,26},{12,28},{14,30},{16,0},... | collective-permute-start | bytes 442376 | tf_op jit(solution)/shard_map/ppermute | solution.py:60
  582.9 55.0 %all-to-all-start.5 = ((f32[16,176,128]{2,1,0:T(8,128)}), f32[16,176,128]{2,1,0:T(8,128)}, u32[]{:S(2)}, u32[]{:S(2)}) async-start(f32[16,176,128]{2,1,0:T(8,128)} %broadcast_in_dim.451), calls=%async_computation.5 | async-start | bytes 2883584 | tf_op jit(solution)/shard_map/all_to_all | solution.py:118
  641.6 41.8 %all-to-all-start.6 = ((f32[16,64,128]{2,1,0:T(8,128)}), f32[16,64,128]{2,1,0:T(8,128)}, u32[]{:S(2)}, u32[]{:S(2)}) async-start(f32[16,64,128]{2,1,0:T(8,128)} %broadcast_in_dim.452), calls=%async_computation.6 | async-start | bytes 1048576 | tf_op jit(solution)/shard_map/all_to_all | solution.py:118
  652.7 27.9 %collective-permute-start.55 = (f32[512,384]{1,0:T(8,128)}, f32[512,384]{1,0:T(8,128)}, u32[]{:S(2)}, u32[]{:S(2)}) collective-permute-start(f32[512,384]{1,0:T(8,128)} %reshape_reshape.14), channel_id=1, source_target_pairs={{0,1},{1,0},{2,3},{3,2},{4,5},{5,4},{6,7},{7,6},{8,9},{9,8},{10,11... | collective-permute-start | bytes 2359304 | tf_op jit(solution)/shard_map/ppermute | solution.py:60
  (147 other events, 1585.8 us)

commit v2 on v1

--- a/solution.py
+++ b/solution.py
@@ -749,10 +749,12 @@
     rows_means = jnp.mean(layer_rows_new, -1)
     ratio = col_stats[local_cols:] / own_layer_cols
     own_share = jnp.stack([jnp.sum(ratio[g * unit : (g + 1) * unit]) for g in range(groups)])
-    shares = gather_list(padded(jnp.concatenate([own_layer_cols, own_share, own_weight_groups]), 1024), "fsdp", inner)
-    layer_cols_new = jnp.concatenate([values[:local_cols] for values in shares])
-    update_groups = jnp.concatenate([values[local_cols : local_cols + groups] for values in shares])
-    weight_groups = jnp.concatenate([values[local_cols + groups : local_cols + 2 * groups] for values in shares])
+    sums_row = jnp.pad(jnp.stack([own_share, own_weight_groups]), ((0, 0), (0, 128 - groups)))
+    share_rows = jnp.concatenate([own_layer_cols.reshape(-1, 128), sums_row], 0)
+    shares = gather_list(share_rows, "fsdp", inner)
+    layer_cols_new = jnp.concatenate([values[:-2] for values in shares], 0).reshape(-1)
+    update_groups = jnp.concatenate([values[-2, :groups] for values in shares])
+    weight_groups = jnp.concatenate([values[-1, :groups] for values in shares])
     counts = MODEL_WIDTH * widths
     spreads = jnp.sqrt(by_block(update_groups) * rows_means / counts)
     layer_scale = (
@@ -787,9 +789,10 @@
     vectors_new, vector_spread = apply_update(norm_vectors, vector_update, vector_square)
     scale_update, scale_moment_new = plain_step(grad_scale, scale_moment)
     log_scale_new, scale_spread = apply_update(log_scale, scale_update, log_scale * log_scale)
-    update_rms = jnp.concatenate(
-        [jnp.stack([embed_spread, head_spread, pos_spread, vector_spread, scale_spread]), spreads]
-    )
+    singles = (embed_spread, head_spread, pos_spread, vector_spread, scale_spread)
+    update_rms = jnp.pad(spreads, (len(singles), 0))
+    for k, single in enumerate(singles):
+        update_rms = jnp.where(jnp.arange(update_rms.shape[0]) == k, single, update_rms)
     return (
         loss_value,
         embedding_new,

time: 704 us -> 709 us (level)
    another operation x1 -> x3, local copies, waits for them, and re-layouts: 0.09 us -> 8.32 us  [by_block(): jnp.stack([jnp.sum(values[..., bounds[b]:bounds[b + 1]], -1) for b in ran...]
where the time goes in v2:
time: 709 us; the launch traced here: 702 us
  waiting for transfers between devices  179 us (25%)
  matrix products  117 us (17%)
  other arithmetic  111 us (16%)
  Pallas kernels  103 us (15%)
  starting transfers between devices  92.5 us (13%)
  local copies, waits for them, and re-layouts  81.2 us (11%)
  between operations  17.5 us (2%)
    ppermute x56, waiting for transfers between devices, swap_by(): return lax.ppermute(values, axis, [(i, i ^ mask) for i in range(size)])  175 us
    dot_general x31, matrix products, dot(): return lax.dot_general(left, right, dims, preferred_element_type=F32)  110 us
    ppermute x56, starting transfers between devices, swap_by(): return lax.ppermute(values, axis, [(i, i ^ mask) for i in range(size)])  52.6 us
    pallas_call x2, Pallas kernels, attend_back(): pl.pallas_call(functools.partial(attention_back_kernel, seq), grid_spec=p...  34.9 us
    pallas_call x1, Pallas kernels, table_update(): pl.pallas_call(table_kernel, grid_spec=pltpu.PrefetchScalarGridSpec(num_s...  29.9 us
    unnamed x290, local copies, waits for them, and re-layouts  22.8 us
    all_to_all x3, starting transfers between devices, everyone(): lax.all_to_all(jnp.broadcast_to(values[None], (size,) + values.shape), ax...  17.5 us
    pallas_call x1, Pallas kernels, attend(): pl.pallas_call(attention_kernel, grid_spec=pltpu.PrefetchScalarGridSpec(n...  16.1 us
  transfers between devices with their start and end apart: 63, of which 24 were waited for; matrix products, arithmetic and copies ran while one was open for 29% of the time, Pallas kernels for 14%

profile of v2, /device:TPU:0, one launch (start us, length us, event | category | flops | bytes accessed | tf_op | source)
XLA Modules:
  0.0 701.8 jit_solution(9039121302570580725)
XLA Ops:
  3.7 8.3 %all-to-all-start = ((s32[16,1,64]{2,1,0:T(1,128)}), s32[16,1,64]{2,1,0:T(1,128)S(1)}, u32[]{:S(2)}, u32[]{:S(2)}) async-start(s32[16,1,64]{2,1,0:T(1,128)} %all_to_all.26), calls=%async_computation | async-start | bytes 16384 | tf_op jit(solution)/shard_map/all_to_all | solution.py:413
  23.8 11.9 %multiply_reduce_fusion = f32[]{:T(128)} fusion(f32[15632,384]{1,0:T(8,128)} %table_ref.3), kind=kLoop, calls=%fused_computation | loop fusion | flops 12005375 | bytes 24010756 | tf_op jit(solution)/shard_map/reduce_sum | solution.py:651
  41.1 14.4 %take_rows.1 = bf16[2048,384]{1,0:T(8,128)(2,1)} custom-call(s32[2048]{0:T(1024)} %reshape.2277.wanted, f32[15632,384]{1,0:T(8,128)} %table_ref.3), custom_call_target="tpu_custom_call" | custom-call | tf_op jit(solution)/shard_map/take_rows/pallas_call | solution.py:224
  55.6 5.8 convert_reduce_fusion
  61.5 5.2 all-to-all-start.1
  83.5 10.9 %collective-permute-done.8 = bf16[2,1,1,1,48,1536]{5,4,0,3,2,1:T(8,128)(2,1)S(1)} collective-permute-done((bf16[2,1,1,1,48,1536]{5,4,0,3,2,1:T(8,128)(2,1)S(1)}, bf16[2,1,1,1,48,1536]{5,4,0,3,2,1:T(8,128)(2,1)S(1)}, u32[]{:S(2)}, u32[]{:S(2)}) %collective-permute-start.8) | collective-permute-done | bytes 294944 | tf_op jit(solution)/shard_map/ppermute | solution.py:60
  97.0 16.4 %collective-permute-done.9 = bf16[2,1,1,2,48,1536]{5,4,0,3,2,1:T(8,128)(2,1)S(1)} collective-permute-done((bf16[2,1,1,2,48,1536]{5,4,0,3,2,1:T(8,128)(2,1)S(1)}, bf16[2,1,1,2,48,1536]{5,4,0,3,2,1:T(8,128)(2,1)S(1)}, u32[]{:S(2)}, u32[]{:S(2)}) %collective-permute-start.9) | collective-permute-done | bytes 589856 | tf_op jit(solution)/shard_map/ppermute | solution.py:60
  117.7 36.7 %collective-permute-done.4 = bf16[2,2,1,1,48,1536]{5,4,3,2,1,0:T(8,128)(2,1)S(1)} collective-permute-done((bf16[2,2,1,1,48,1536]{5,4,3,2,1,0:T(8,128)(2,1)S(1)}, bf16[2,2,1,1,48,1536]{5,4,3,2,1,0:T(8,128)(2,1)S(1)}, u32[]{:S(2)}, u32[]{:S(2)}) %collective-permute-start.4) | collective-permute-done | bytes 589856 | tf_op jit(solution)/shard_map/ppermute | solution.py:60
  161.6 20.8 %collective-permute-done.5 = bf16[2,2,2,1,48,1536]{5,4,3,2,1,0:T(8,128)(2,1)} collective-permute-done((bf16[2,2,2,1,48,1536]{5,4,3,2,1,0:T(8,128)(2,1)}, bf16[2,2,2,1,48,1536]{5,4,3,2,1,0:T(8,128)(2,1)}, u32[]{:S(2)}, u32[]{:S(2)}) %collective-permute-start.5) | collective-permute-done | bytes 1179680 | tf_op jit(solution)/shard_map/ppermute | solution.py:60
  188.0 4.3 maximum_select_fusion.2
  206.1 4.0 add_convert_fusion.q_ref.k_ref
  210.2 16.1 %attend.1 = bf16[1024,768]{1,0:T(8,128)(2,1)} custom-call(s32[2]{0:T(128)} %lengths.2, bf16[1024,1536]{1,0:T(8,128)(2,1)} %add_convert_fusion.q_ref.k_ref, bf16[1024,1536]{1,0:T(8,128)(2,1)} %add_convert_fusion.q_ref.k_ref, bf16[1024,768]{1,0:T(8,128)(2,1)} %add_convert_fusion.1.v_ref), custom_call_target="tpu_custom_call" | custom-call | tf_op jit(solution)/shard_map/attend/pallas_call | solution.py:150
  233.1 5.4 multiply_convert_fusion
  238.5 7.0 multiply_convert_fusion.1
  245.5 5.4 fusion.82
  251.0 4.9 fusion.186
  258.3 6.0 all-to-all-start.2
  268.4 4.9 all-to-all-done.2
  274.0 8.0 %contrast.1 = (f32[64,768]{1,0:T(8,128)}, f32[64,768]{1,0:T(8,128)}, f32[8,128]{1,0:T(8,128)}) custom-call(f32[1]{0:T(128)} %bitcast.405.scale_ref, f32[64,768]{1,0:T(8,128)} %reshape.2283.pooled_ref, f32[768,768]{1,0:T(8,128)} %head_ref.1), custom_call_target="tpu_custom_call" | custom-call | tf_op jit(solution)/shard_map/contrast/pallas_call | solution.py:340
  288.2 4.1 convolution_convert_fusion
  292.2 6.9 fusion.187
  299.2 6.9 fusion.188
  306.1 4.4 convolution_convert_fusion.1
  310.5 4.5 fusion.76
  327.1 17.4 %shard_map.338 = (bf16[1024,768]{1,0:T(8,128)(2,1)}, bf16[1024,768]{1,0:T(8,128)(2,1)}, bf16[1024,768]{1,0:T(8,128)(2,1)}, f32[16,768]{1,0:T(8,128)}) custom-call(s32[2]{0:T(128)} %lengths.2, bf16[1024,1536]{1,0:T(8,128)(2,1)} %add_convert_fusion.q_ref.k_ref, bf16[1024,1536]{1,0:T(8,128)(2,1)} %add_convert_fusion.q_ref.k_ref, ...), custom_call_target="tpu_custom_call" | custom-call | tf_op jit(solution)/shard_map/pallas_call | solution.py:196
  344.5 17.5 %shard_map.339 = (bf16[1024,768]{1,0:T(8,128)(2,1)}, bf16[1024,768]{1,0:T(8,128)(2,1)}, bf16[1024,768]{1,0:T(8,128)(2,1)}, f32[16,768]{1,0:T(8,128)}) custom-call(s32[2]{0:T(128)} %lengths.2, bf16[1024,1536]{1,0:T(8,128)(2,1)} %add_convert_fusion.q_ref.k_ref, ...), custom_call_target="tpu_custom_call", output_to_operand_aliasing={{0}: (5, {}), {1}: (6, {}), {2}: (7, {}), {3}: (8, {})} | custom-call | tf_op jit(solution)/shard_map/pallas_call | solution.py:196
  407.0 3.9 collective-permute-done.39
  414.0 4.8 all-to-all-start.3
  430.8 7.5 %collective-permute-done.26 = bf16[8,48,384]{2,1,0:T(8,128)(2,1)S(1)} collective-permute-done((bf16[8,48,384]{2,1,0:T(8,128)(2,1)S(1)}, bf16[8,48,384]{2,1,0:T(8,128)(2,1)S(1)}, u32[]{:S(2)}, u32[]{:S(2)}) %collective-permute-start.26) | collective-permute-done | bytes 294944 | tf_op jit(solution)/shard_map/ppermute | solution.py:60
  439.5 11.9 %collective-permute-done.31 = bf16[8,48,384]{2,1,0:T(8,128)(2,1)S(1)} collective-permute-done((bf16[8,48,384]{2,1,0:T(8,128)(2,1)S(1)}, bf16[8,48,384]{2,1,0:T(8,128)(2,1)S(1)}, u32[]{:S(2)}, u32[]{:S(2)}) %collective-permute-start.31) | collective-permute-done | bytes 294944 | tf_op jit(solution)/shard_map/ppermute | solution.py:60
  467.2 5.1 collective-permute-done.23
  478.3 5.4 convert_add_fusion.1
  486.3 4.3 convert_add_fusion
  494.4 17.9 %collective-permute-done.42 = bf16[384,1536]{1,0:T(8,128)(2,1)S(1)} collective-permute-done((bf16[384,1536]{1,0:T(8,128)(2,1)S(1)}, bf16[384,1536]{1,0:T(8,128)(2,1)S(1)}, u32[]{:S(2)}, u32[]{:S(2)}) %collective-permute-start.42) | collective-permute-done | bytes 1179680 | tf_op jit(solution)/shard_map/ppermute | solution.py:60
  514.6 4.7 collective-permute-done.47
  520.8 6.2 multiply_reduce_fusion.5
  534.5 4.0 all-to-all-start.4
  538.5 6.4 collective-permute-done.43
  549.8 5.8 collective-permute-done.44
  558.9 9.3 %collective-permute-done.45 = bf16[48,1536]{1,0:T(8,128)(2,1)S(1)} collective-permute-done((bf16[48,1536]{1,0:T(8,128)(2,1)S(1)}, bf16[48,1536]{1,0:T(8,128)(2,1)S(1)}, u32[]{:S(2)}, u32[]{:S(2)}) %collective-permute-start.45) | collective-permute-done | bytes 147488 | tf_op jit(solution)/shard_map/ppermute | solution.py:60
  577.8 3.9 concatenate.677
  582.9 4.7 all-to-all-start.5
  587.7 4.6 multiply_reduce_fusion.17
  607.3 29.9 %table_update.1 = (f32[15632,384]{1,0:T(8,128)}, bf16[15632,384]{1,0:T(8,128)(2,1)}) custom-call(s32[2048]{0:T(1024)} %copy-done.55, s32[9]{0:T(128)} %convert_reduce_fusion.1.starts, f32[15632,384]{1,0:T(8,128)} %table_ref.3, f32[2048,384]{1,0:T(8,128)} %get-tuple-element.255.update_ref, f32[1,384]{1,0:T(1,128)} %broadcast_in_dim.451.scale_ref), custom_call_target="tpu_custom_call" | custom-call | tf_op jit(solution)/shard_map/table_update/pallas_call | solution.py:256
  641.8 6.8 all-to-all-start.6
  654.4 4.0 stack.158
  669.8 3.8 stack.164
  673.6 4.4 stack.167
  (674 shorter events, 266.9 us)
Async XLA Ops:
  3.7 32.6 %all-to-all-start = ((s32[16,1,64]{2,1,0:T(1,128)}), s32[16,1,64]{2,1,0:T(1,128)S(1)}, u32[]{:S(2)}, u32[]{:S(2)}) async-start(s32[16,1,64]{2,1,0:T(1,128)} %all_to_all.26), calls=%async_computation | async-start | bytes 16384 | tf_op jit(solution)/shard_map/all_to_all | solution.py:413
  14.0 62.3 %collective-permute-start.7 = (bf16[1,1,1,1,48,1536]{5,4,0,3,2,1:T(8,128)(2,1)}, bf16[1,1,1,1,48,1536]{5,4,0,3,2,1:T(8,128)(2,1)S(1)}, u32[]{:S(2)}, u32[]{:S(2)}) collective-permute-start(bf16[1,1,1,1,48,1536]{5,4,0,3,2,1:T(8,128)(2,1)} %get-tuple-element.280), channel_id=1, source_target_pairs={{0,16},{2,18},{4,20},{6,22},{8,24},{10,26},{12,28},{14,30},{16,0},... | collective-permute-start | bytes 442376 | tf_op jit(solution)/shard_map/ppermute | solution.py:60
  16.8 62.5 %collective-permute-start.2 = (bf16[1,1,1,1,48,1536]{5,4,3,2,1,0:T(8,128)(2,1)}, bf16[1,1,1,1,48,1536]{5,4,3,2,1,0:T(8,128)(2,1)S(1)}, u32[]{:S(2)}, u32[]{:S(2)}) collective-permute-start(bf16[1,1,1,1,48,1536]{5,4,3,2,1,0:T(8,128)(2,1)} %get-tuple-element.279), channel_id=1, source_target_pairs={{0,16},{2,18},{4,20},{6,22},{8,24},{10,26},{12,28},{14,30},{16,0},... | collective-permute-start | bytes 442376 | tf_op jit(solution)/shard_map/ppermute | solution.py:60
  16.9 65.0 %collective-permute-start.12 = (bf16[1,1,1,1,48,1536]{5,4,3,2,1,0:T(8,128)(2,1)S(1)}, bf16[1,1,1,1,48,1536]{5,4,3,2,1,0:T(8,128)(2,1)S(1)}, u32[]{:S(2)}, u32[]{:S(2)}) collective-permute-start(bf16[1,1,1,1,48,1536]{5,4,3,2,1,0:T(8,128)(2,1)S(1)} %get-tuple-element.278), channel_id=1, source_target_pairs={{0,16},{2,18},{4,20},{6,22},{8,24},{10,26},{12,28},{14,30},{16,0},... | collective-permute-start | bytes 442376 | tf_op jit(solution)/shard_map/ppermute | solution.py:60
  61.5 99.7 %all-to-all-start.1 = ((bf16[16,2,64,384]{3,2,1,0:T(8,128)(2,1)}), bf16[16,2,64,384]{3,2,1,0:T(8,128)(2,1)S(1)}, u32[]{:S(2)}, u32[]{:S(2)}) async-start(bf16[16,2,64,384]{3,2,1,0:T(8,128)(2,1)} %bitcast.417), calls=%async_computation.1 | async-start | bytes 3145728 | tf_op jit(solution)/shard_map/all_to_all | solution.py:441
  77.4 17.0 %collective-permute-start.8 = (bf16[2,1,1,1,48,1536]{5,4,0,3,2,1:T(8,128)(2,1)S(1)}, bf16[2,1,1,1,48,1536]{5,4,0,3,2,1:T(8,128)(2,1)S(1)}, u32[]{:S(2)}, u32[]{:S(2)}) collective-permute-start(bf16[2,1,1,1,48,1536]{5,4,0,3,2,1:T(8,128)(2,1)S(1)} %maximum_select_fusion.13), channel_id=1, source_target_pairs={{0,2},{2,0},{4,6},{6,4},{8,10},{10,8},{12,14},{14,12},{16,18},{18,... | collective-permute-start | bytes 884744 | tf_op jit(solution)/shard_map/ppermute | solution.py:60
  80.4 35.8 %collective-permute-start.3 = (bf16[2,1,1,1,48,1536]{5,4,3,2,1,0:T(8,128)(2,1)S(1)}, bf16[2,1,1,1,48,1536]{5,4,3,2,1,0:T(8,128)(2,1)S(1)}, u32[]{:S(2)}, u32[]{:S(2)}) collective-permute-start(bf16[2,1,1,1,48,1536]{5,4,3,2,1,0:T(8,128)(2,1)S(1)} %bitcast_select_fusion.1), channel_id=1, source_target_pairs={{0,8},{2,10},{4,12},{6,14},{8,0},{10,2},{12,4},{14,6},{16,24},{18,... | collective-permute-start | bytes 884744 | tf_op jit(solution)/shard_map/ppermute | solution.py:60
  82.0 34.4 %collective-permute-start.13 = (bf16[2,1,1,1,48,1536]{5,4,3,2,1,0:T(8,128)(2,1)S(1)}, bf16[2,1,1,1,48,1536]{5,4,3,2,1,0:T(8,128)(2,1)S(1)}, u32[]{:S(2)}, u32[]{:S(2)}) collective-permute-start(bf16[2,1,1,1,48,1536]{5,4,3,2,1,0:T(8,128)(2,1)S(1)} %bitcast_select_fusion), channel_id=1, source_target_pairs={{0,4},{2,6},{4,0},{6,2},{8,12},{10,14},{12,8},{14,10},{16,20},{18,... | collective-permute-start | bytes 884744 | tf_op jit(solution)/shard_map/ppermute | solution.py:60
  94.5 18.9 %collective-permute-start.9 = (bf16[2,1,1,2,48,1536]{5,4,0,3,2,1:T(8,128)(2,1)S(1)}, bf16[2,1,1,2,48,1536]{5,4,0,3,2,1:T(8,128)(2,1)S(1)}, u32[]{:S(2)}, u32[]{:S(2)}) collective-permute-start(bf16[2,1,1,2,48,1536]{5,4,0,3,2,1:T(8,128)(2,1)S(1)} %maximum_select_fusion.9), channel_id=1, source_target_pairs={{0,8},{2,10},{4,12},{6,14},{8,0},{10,2},{12,4},{14,6},{16,24},{18,... | collective-permute-start | bytes 1769480 | tf_op jit(solution)/shard_map/ppermute | solution.py:60
  113.6 42.6 %collective-permute-start.10 = (bf16[2,2,1,2,48,1536]{5,4,0,3,2,1:T(8,128)(2,1)S(1)}, bf16[2,2,1,2,48,1536]{5,4,0,3,2,1:T(8,128)(2,1)S(1)}, u32[]{:S(2)}, u32[]{:S(2)}) collective-permute-start(bf16[2,2,1,2,48,1536]{5,4,0,3,2,1:T(8,128)(2,1)S(1)} %maximum_select_fusion.4), channel_id=1, source_target_pairs={{0,4},{2,6},{4,0},{6,2},{8,12},{10,14},{12,8},{14,10},{16,20},{18,... | collective-permute-start | bytes 3538952 | tf_op jit(solution)/shard_map/ppermute | solution.py:60
  116.2 38.1 %collective-permute-start.4 = (bf16[2,2,1,1,48,1536]{5,4,3,2,1,0:T(8,128)(2,1)S(1)}, bf16[2,2,1,1,48,1536]{5,4,3,2,1,0:T(8,128)(2,1)S(1)}, u32[]{:S(2)}, u32[]{:S(2)}) collective-permute-start(bf16[2,2,1,1,48,1536]{5,4,3,2,1,0:T(8,128)(2,1)S(1)} %maximum_select_fusion.7), channel_id=1, source_target_pairs={{0,4},{2,6},{4,0},{6,2},{8,12},{10,14},{12,8},{14,10},{16,20},{18,... | collective-permute-start | bytes 1769480 | tf_op jit(solution)/shard_map/ppermute | solution.py:60
  116.5 41.7 %collective-permute-start.14 = (bf16[2,1,2,1,48,1536]{5,4,3,2,1,0:T(8,128)(2,1)S(1)}, bf16[2,1,2,1,48,1536]{5,4,3,2,1,0:T(8,128)(2,1)S(1)}, u32[]{:S(2)}, u32[]{:S(2)}) collective-permute-start(bf16[2,1,2,1,48,1536]{5,4,3,2,1,0:T(8,128)(2,1)S(1)} %maximum_select_fusion.11), channel_id=1, source_target_pairs={{0,2},{2,0},{4,6},{6,4},{8,10},{10,8},{12,14},{14,12},{16,18},{18,... | collective-permute-start | bytes 1769480 | tf_op jit(solution)/shard_map/ppermute | solution.py:60
  155.5 27.0 %collective-permute-start.5 = (bf16[2,2,2,1,48,1536]{5,4,3,2,1,0:T(8,128)(2,1)}, bf16[2,2,2,1,48,1536]{5,4,3,2,1,0:T(8,128)(2,1)}, u32[]{:S(2)}, u32[]{:S(2)}) collective-permute-start(bf16[2,2,2,1,48,1536]{5,4,3,2,1,0:T(8,128)(2,1)} %maximum_select_fusion.3), channel_id=1, source_target_pairs={{0,2},{2,0},{4,6},{6,4},{8,10},{10,8},{12,14},{14,12},{16,18},{18,... | collective-permute-start | bytes 3538952 | tf_op jit(solution)/shard_map/ppermute | solution.py:60
  158.2 40.1 %collective-permute-start.11 = (bf16[768,1536]{1,0:T(8,128)(2,1)}, bf16[768,1536]{1,0:T(8,128)(2,1)}, u32[]{:S(2)}, u32[]{:S(2)}) collective-permute-start(bf16[768,1536]{1,0:T(8,128)(2,1)} %bitcast.26), channel_id=1, source_target_pairs={{0,1},{1,0},{2,3},{3,2},{4,5},{5,4},{6,7},{7,6},{8,9},{9,8},{10,11... | collective-permute-start | bytes 7077896 | tf_op jit(solution)/shard_map/ppermute | solution.py:60
  159.3 28.7 %collective-permute-start.15 = (bf16[2,1,2,2,48,1536]{5,4,3,2,1,0:T(8,128)(2,1)}, bf16[2,1,2,2,48,1536]{5,4,3,2,1,0:T(8,128)(2,1)}, u32[]{:S(2)}, u32[]{:S(2)}) collective-permute-start(bf16[2,1,2,2,48,1536]{5,4,3,2,1,0:T(8,128)(2,1)} %maximum_select_fusion.5), channel_id=1, source_target_pairs={{0,8},{2,10},{4,12},{6,14},{8,0},{10,2},{12,4},{14,6},{16,24},{18,... | collective-permute-start | bytes 3538952 | tf_op jit(solution)/shard_map/ppermute | solution.py:60
  161.3 31.0 %collective-permute-start.1 = (bf16[1024,384]{1,0:T(8,128)(2,1)S(1)}, bf16[1024,384]{1,0:T(8,128)(2,1)S(1)}, u32[]{:S(2)}, u32[]{:S(2)}) collective-permute-start(bf16[1024,384]{1,0:T(8,128)(2,1)S(1)} %bitcast.465), channel_id=1, source_target_pairs={{0,1},{1,0},{2,3},{3,2},{4,5},{5,4},{6,7},{7,6},{8,9},{9,8},{10,11... | collective-permute-start | bytes 2359304 | tf_op jit(solution)/shard_map/ppermute | solution.py:60
  185.4 17.9 %collective-permute-start.6 = (bf16[768,1536]{1,0:T(8,128)(2,1)S(1)}, bf16[768,1536]{1,0:T(8,128)(2,1)S(1)}, u32[]{:S(2)}, u32[]{:S(2)}) collective-permute-start(bf16[768,1536]{1,0:T(8,128)(2,1)S(1)} %bitcast.407), channel_id=1, source_target_pairs={{0,1},{1,0},{2,3},{3,2},{4,5},{5,4},{6,7},{7,6},{8,9},{9,8},{10,11... | collective-permute-start | bytes 7077896 | tf_op jit(solution)/shard_map/ppermute | solution.py:60
  192.3 46.2 %collective-permute-start.16 = (bf16[768,1536]{1,0:T(8,128)(2,1)}, bf16[768,1536]{1,0:T(8,128)(2,1)}, u32[]{:S(2)}, u32[]{:S(2)}) collective-permute-start(bf16[768,1536]{1,0:T(8,128)(2,1)} %bitcast.37), channel_id=1, source_target_pairs={{0,1},{1,0},{2,3},{3,2},{4,5},{5,4},{6,7},{7,6},{8,9},{9,8},{10,11... | collective-permute-start | bytes 7077896 | tf_op jit(solution)/shard_map/ppermute | solution.py:60
  258.3 15.0 %all-to-all-start.2 = ((f32[32,2,768]{2,1,0:T(2,128)}), f32[32,2,768]{2,1,0:T(2,128)S(1)}, u32[]{:S(2)}, u32[]{:S(2)}) async-start(f32[32,2,768]{2,1,0:T(2,128)} %broadcast_in_dim.395), calls=%async_computation.2 | async-start | bytes 393216 | tf_op jit(solution)/shard_map/all_to_all | solution.py:118
  326.0 54.1 %collective-permute-start.36 = (bf16[768,384]{1,0:T(8,128)(2,1)}, bf16[768,384]{1,0:T(8,128)(2,1)}, u32[]{:S(2)}, u32[]{:S(2)}) collective-permute-start(bf16[768,384]{1,0:T(8,128)(2,1)} %convolution_convert_fusion.3), channel_id=1, source_target_pairs={{0,1},{1,0},{2,3},{3,2},{4,5},{5,4},{6,7},{7,6},{8,9},{9,8},{10,11... | collective-permute-start | bytes 1769480 | tf_op jit(solution)/shard_map/ppermute | solution.py:60
  326.6 151.7 %collective-permute-start.41 = (bf16[768,1536]{1,0:T(8,128)(2,1)}, bf16[768,1536]{1,0:T(8,128)(2,1)}, u32[]{:S(2)}, u32[]{:S(2)}) collective-permute-start(bf16[768,1536]{1,0:T(8,128)(2,1)} %convolution_convert_fusion.1), channel_id=1, source_target_pairs={{0,1},{1,0},{2,3},{3,2},{4,5},{5,4},{6,7},{7,6},{8,9},{9,8},{10,11... | collective-permute-start | bytes 7077896 | tf_op jit(solution)/shard_map/ppermute | solution.py:60
  326.6 158.2 %collective-permute-start.46 = (bf16[768,1536]{1,0:T(8,128)(2,1)}, bf16[768,1536]{1,0:T(8,128)(2,1)}, u32[]{:S(2)}, u32[]{:S(2)}) collective-permute-start(bf16[768,1536]{1,0:T(8,128)(2,1)} %convolution_convert_fusion), channel_id=1, source_target_pairs={{0,1},{1,0},{2,3},{3,2},{4,5},{5,4},{6,7},{7,6},{8,9},{9,8},{10,11... | collective-permute-start | bytes 7077896 | tf_op jit(solution)/shard_map/ppermute | solution.py:60
  375.6 9.3 %collective-permute-start.17 = (bf16[1024,384]{1,0:T(8,128)(2,1)}, bf16[1024,384]{1,0:T(8,128)(2,1)}, u32[]{:S(2)}, u32[]{:S(2)}) collective-permute-start(bf16[1024,384]{1,0:T(8,128)(2,1)} %get-tuple-element.265), channel_id=1, source_target_pairs={{0,1},{1,0},{2,3},{3,2},{4,5},{5,4},{6,7},{7,6},{8,9},{9,8},{10,11... | collective-permute-start | bytes 2359304 | tf_op jit(solution)/shard_map/ppermute | solution.py:60
  383.0 16.4 %collective-permute-start.37 = (bf16[384,384]{1,0:T(8,128)(2,1)S(1)}, bf16[384,384]{1,0:T(8,128)(2,1)}, u32[]{:S(2)}, u32[]{:S(2)}) collective-permute-start(bf16[384,384]{1,0:T(8,128)(2,1)S(1)} %bitcast.481), channel_id=1, source_target_pairs={{0,8},{2,10},{4,12},{6,14},{8,0},{10,2},{12,4},{14,6},{16,24},{18,... | collective-permute-start | bytes 884744 | tf_op jit(solution)/shard_map/ppermute | solution.py:60
  389.2 31.9 %collective-permute-start.25 = (bf16[768,384]{1,0:T(8,128)(2,1)}, bf16[768,384]{1,0:T(8,128)(2,1)}, u32[]{:S(2)}, u32[]{:S(2)}) collective-permute-start(bf16[768,384]{1,0:T(8,128)(2,1)} %convolution_convert_fusion.5), channel_id=1, source_target_pairs={{0,1},{1,0},{2,3},{3,2},{4,5},{5,4},{6,7},{7,6},{8,9},{9,8},{10,11... | collective-permute-start | bytes 1769480 | tf_op jit(solution)/shard_map/ppermute | solution.py:60
  394.5 25.1 %collective-permute-start.20 = (bf16[512,384]{1,0:T(8,128)(2,1)}, bf16[512,384]{1,0:T(8,128)(2,1)}, u32[]{:S(2)}, u32[]{:S(2)}) collective-permute-start(bf16[512,384]{1,0:T(8,128)(2,1)} %dynamic-slice_convert_fusion.4), channel_id=1, source_target_pairs={{0,1},{1,0},{2,3},{3,2},{4,5},{5,4},{6,7},{7,6},{8,9},{9,8},{10,11... | collective-permute-start | bytes 1179656 | tf_op jit(solution)/shard_map/ppermute | solution.py:60
  410.9 7.9 %collective-permute-start.40 = (bf16[48,384]{1,0:T(8,128)(2,1)S(1)}, bf16[48,384]{1,0:T(8,128)(2,1)S(1)}, u32[]{:S(2)}, u32[]{:S(2)}) collective-permute-start(bf16[48,384]{1,0:T(8,128)(2,1)S(1)} %fusion.130), channel_id=1, source_target_pairs={{0,16},{2,18},{4,20},{6,22},{8,24},{10,26},{12,28},{14,30},{16,0},... | collective-permute-start | bytes 110600 | tf_op jit(solution)/shard_map/ppermute | solution.py:60
  414.0 105.8 %all-to-all-start.3 = ((bf16[16,2,64,384]{3,2,1,0:T(8,128)(2,1)}), bf16[16,2,64,384]{3,2,1,0:T(8,128)(2,1)}, u32[]{:S(2)}, u32[]{:S(2)}) async-start(bf16[16,2,64,384]{3,2,1,0:T(8,128)(2,1)} %pad_maximum_fusion), calls=%async_computation.3 | async-start | bytes 3145728 | tf_op jit(solution)/shard_map/all_to_all | solution.py:580
  419.5 8.6 %collective-permute-start.19 = (bf16[768,384]{1,0:T(8,128)(2,1)}, bf16[768,384]{1,0:T(8,128)(2,1)S(1)}, u32[]{:S(2)}, u32[]{:S(2)}) collective-permute-start(bf16[768,384]{1,0:T(8,128)(2,1)} %convolution_convert_fusion.6), channel_id=1, source_target_pairs={{0,1},{1,0},{2,3},{3,2},{4,5},{5,4},{6,7},{7,6},{8,9},{9,8},{10,11... | collective-permute-start | bytes 1769480 | tf_op jit(solution)/shard_map/ppermute | solution.py:60
  423.6 14.7 %collective-permute-start.26 = (bf16[8,48,384]{2,1,0:T(8,128)(2,1)S(1)}, bf16[8,48,384]{2,1,0:T(8,128)(2,1)S(1)}, u32[]{:S(2)}, u32[]{:S(2)}) collective-permute-start(bf16[8,48,384]{2,1,0:T(8,128)(2,1)S(1)} %bitcast.479), channel_id=1, source_target_pairs={{0,4},{2,6},{4,0},{6,2},{8,12},{10,14},{12,8},{14,10},{16,20},{18,... | collective-permute-start | bytes 884744 | tf_op jit(solution)/shard_map/ppermute | solution.py:60
  426.6 24.9 %collective-permute-start.31 = (bf16[8,48,384]{2,1,0:T(8,128)(2,1)S(1)}, bf16[8,48,384]{2,1,0:T(8,128)(2,1)S(1)}, u32[]{:S(2)}, u32[]{:S(2)}) collective-permute-start(bf16[8,48,384]{2,1,0:T(8,128)(2,1)S(1)} %bitcast.480), channel_id=1, source_target_pairs={{0,8},{2,10},{4,12},{6,14},{8,0},{10,2},{12,4},{14,6},{16,24},{18,... | collective-permute-start | bytes 884744 | tf_op jit(solution)/shard_map/ppermute | solution.py:60
  429.2 31.0 %collective-permute-start.21 = (bf16[8,80,384]{2,1,0:T(8,128)(2,1)S(1)}, bf16[8,80,384]{2,1,0:T(8,128)(2,1)S(1)}, u32[]{:S(2)}, u32[]{:S(2)}) collective-permute-start(bf16[8,80,384]{2,1,0:T(8,128)(2,1)S(1)} %fusion.110), channel_id=1, source_target_pairs={{0,2},{2,0},{4,6},{6,4},{8,10},{10,8},{12,14},{14,12},{16,18},{18,... | collective-permute-start | bytes 1474568 | tf_op jit(solution)/shard_map/ppermute | solution.py:60
  438.4 15.2 %collective-permute-start.27 = (bf16[4,48,384]{2,1,0:T(8,128)(2,1)S(1)}, bf16[4,48,384]{2,1,0:T(8,128)(2,1)S(1)}, u32[]{:S(2)}, u32[]{:S(2)}) collective-permute-start(bf16[4,48,384]{2,1,0:T(8,128)(2,1)S(1)} %bitcast.484), channel_id=1, source_target_pairs={{0,8},{2,10},{4,12},{6,14},{8,0},{10,2},{12,4},{14,6},{16,24},{18,... | collective-permute-start | bytes 442376 | tf_op jit(solution)/shard_map/ppermute | solution.py:60
  453.6 6.8 collective-permute-start.28
  463.4 11.1 %collective-permute-start.34 = (bf16[1,48,384]{2,1,0:T(8,128)(2,1)S(1)}, bf16[1,48,384]{2,1,0:T(8,128)(2,1)S(1)}, u32[]{:S(2)}, u32[]{:S(2)}) collective-permute-start(bf16[1,48,384]{2,1,0:T(8,128)(2,1)S(1)} %dynamic-slice_convert_fusion.20), channel_id=1, source_target_pairs={{0,16},{2,18},{4,20},{6,22},{8,24},{10,26},{12,28},{14,30},{16,0},... | collective-permute-start | bytes 110600 | tf_op jit(solution)/shard_map/ppermute | solution.py:60
  477.6 14.8 %collective-permute-start.35 = (f32[48,1152]{1,0:T(8,128)S(1)}, f32[48,1152]{1,0:T(8,128)S(1)}, u32[]{:S(2)}, u32[]{:S(2)}) collective-permute-start(f32[48,1152]{1,0:T(8,128)S(1)} %pad_maximum_fusion.4), channel_id=1, source_target_pairs={{0,1},{1,0},{2,3},{3,2},{4,5},{5,4},{6,7},{7,6},{8,9},{9,8},{10,11... | collective-permute-start | bytes 663560 | tf_op jit(solution)/shard_map/ppermute | solution.py:60
  483.9 28.4 %collective-permute-start.42 = (bf16[384,1536]{1,0:T(8,128)(2,1)S(1)}, bf16[384,1536]{1,0:T(8,128)(2,1)S(1)}, u32[]{:S(2)}, u32[]{:S(2)}) collective-permute-start(bf16[384,1536]{1,0:T(8,128)(2,1)S(1)} %bitcast.454), channel_id=1, source_target_pairs={{0,4},{2,6},{4,0},{6,2},{8,12},{10,14},{12,8},{14,10},{16,20},{18,... | collective-permute-start | bytes 3538952 | tf_op jit(solution)/shard_map/ppermute | solution.py:60
  490.9 28.4 %collective-permute-start.47 = (bf16[384,1536]{1,0:T(8,128)(2,1)S(1)}, bf16[384,1536]{1,0:T(8,128)(2,1)S(1)}, u32[]{:S(2)}, u32[]{:S(2)}) collective-permute-start(bf16[384,1536]{1,0:T(8,128)(2,1)S(1)} %bitcast.455), channel_id=1, source_target_pairs={{0,2},{2,0},{4,6},{6,4},{8,10},{10,8},{12,14},{14,12},{16,18},{18,... | collective-permute-start | bytes 3538952 | tf_op jit(solution)/shard_map/ppermute | solution.py:60
  528.0 16.9 %collective-permute-start.43 = (bf16[192,1536]{1,0:T(8,128)(2,1)}, bf16[192,1536]{1,0:T(8,128)(2,1)}, u32[]{:S(2)}, u32[]{:S(2)}) collective-permute-start(bf16[192,1536]{1,0:T(8,128)(2,1)} %bitcast.100), channel_id=1, source_target_pairs={{0,2},{2,0},{4,6},{6,4},{8,10},{10,8},{12,14},{14,12},{16,18},{18,... | collective-permute-start | bytes 1769480 | tf_op jit(solution)/shard_map/ppermute | solution.py:60
  529.4 18.5 %collective-permute-start.48 = (bf16[192,1536]{1,0:T(8,128)(2,1)}, bf16[192,1536]{1,0:T(8,128)(2,1)}, u32[]{:S(2)}, u32[]{:S(2)}) collective-permute-start(bf16[192,1536]{1,0:T(8,128)(2,1)} %bitcast.112), channel_id=1, source_target_pairs={{0,8},{2,10},{4,12},{6,14},{8,0},{10,2},{12,4},{14,6},{16,24},{18,... | collective-permute-start | bytes 1769480 | tf_op jit(solution)/shard_map/ppermute | solution.py:60
  534.5 37.9 %all-to-all-start.4 = ((f32[32,16,128]{2,1,0:T(8,128)}), f32[32,16,128]{2,1,0:T(8,128)}, u32[]{:S(2)}, u32[]{:S(2)}) async-start(f32[32,16,128]{2,1,0:T(8,128)} %bitcast.192), calls=%async_computation.4 | async-start | bytes 524288 | tf_op jit(solution)/shard_map/all_to_all | solution.py:671
  546.2 9.4 %collective-permute-start.44 = (bf16[96,1536]{1,0:T(8,128)(2,1)S(1)}, bf16[96,1536]{1,0:T(8,128)(2,1)S(1)}, u32[]{:S(2)}, u32[]{:S(2)}) collective-permute-start(bf16[96,1536]{1,0:T(8,128)(2,1)S(1)} %bitcast.482), channel_id=1, source_target_pairs={{0,8},{2,10},{4,12},{6,14},{8,0},{10,2},{12,4},{14,6},{16,24},{18,... | collective-permute-start | bytes 884744 | tf_op jit(solution)/shard_map/ppermute | solution.py:60
  549.2 8.3 %collective-permute-start.49 = (bf16[96,1536]{1,0:T(8,128)(2,1)S(1)}, bf16[96,1536]{1,0:T(8,128)(2,1)S(1)}, u32[]{:S(2)}, u32[]{:S(2)}) collective-permute-start(bf16[96,1536]{1,0:T(8,128)(2,1)S(1)} %bitcast.483), channel_id=1, source_target_pairs={{0,4},{2,6},{4,0},{6,2},{8,12},{10,14},{12,8},{14,10},{16,20},{18,... | collective-permute-start | bytes 884744 | tf_op jit(solution)/shard_map/ppermute | solution.py:60
  555.7 12.5 %collective-permute-start.45 = (bf16[48,1536]{1,0:T(8,128)(2,1)S(1)}, bf16[48,1536]{1,0:T(8,128)(2,1)S(1)}, u32[]{:S(2)}, u32[]{:S(2)}) collective-permute-start(bf16[48,1536]{1,0:T(8,128)(2,1)S(1)} %fusion.115), channel_id=1, source_target_pairs={{0,16},{2,18},{4,20},{6,22},{8,24},{10,26},{12,28},{14,30},{16,0},... | collective-permute-start | bytes 442376 | tf_op jit(solution)/shard_map/ppermute | solution.py:60
  557.5 13.7 %collective-permute-start.50 = (bf16[48,1536]{1,0:T(8,128)(2,1)S(1)}, bf16[48,1536]{1,0:T(8,128)(2,1)S(1)}, u32[]{:S(2)}, u32[]{:S(2)}) collective-permute-start(bf16[48,1536]{1,0:T(8,128)(2,1)S(1)} %fusion.116), channel_id=1, source_target_pairs={{0,16},{2,18},{4,20},{6,22},{8,24},{10,26},{12,28},{14,30},{16,0},... | collective-permute-start | bytes 442376 | tf_op jit(solution)/shard_map/ppermute | solution.py:60
  582.9 54.4 %all-to-all-start.5 = ((f32[16,176,128]{2,1,0:T(8,128)}), f32[16,176,128]{2,1,0:T(8,128)}, u32[]{:S(2)}, u32[]{:S(2)}) async-start(f32[16,176,128]{2,1,0:T(8,128)} %broadcast_in_dim.464), calls=%async_computation.5 | async-start | bytes 2883584 | tf_op jit(solution)/shard_map/all_to_all | solution.py:118
  641.8 46.7 %all-to-all-start.6 = ((f32[16,64,128]{2,1,0:T(8,128)}), f32[16,64,128]{2,1,0:T(8,128)}, u32[]{:S(2)}, u32[]{:S(2)}) async-start(f32[16,64,128]{2,1,0:T(8,128)} %broadcast_in_dim.465), calls=%async_computation.6 | async-start | bytes 1048576 | tf_op jit(solution)/shard_map/all_to_all | solution.py:118
  653.0 32.7 %collective-permute-start.55 = (f32[512,384]{1,0:T(8,128)}, f32[512,384]{1,0:T(8,128)}, u32[]{:S(2)}, u32[]{:S(2)}) collective-permute-start(f32[512,384]{1,0:T(8,128)} %reshape_reshape.14), channel_id=1, source_target_pairs={{0,1},{1,0},{2,3},{3,2},{4,5},{5,4},{6,7},{7,6},{8,9},{9,8},{10,11... | collective-permute-start | bytes 2359304 | tf_op jit(solution)/shard_map/ppermute | solution.py:60
  (146 other events, 1597.4 us)
